TPU v7x, 32 devices: a whole 2x2x4 slice. The times are simulated.
32 devices in a mesh: group: 2 (over x), circ: 16 (over z, y, core).
Axes of the slice: x: 2, y: 2, z: 4, core: 2. Of those that a mesh axis runs over, the one named last changes fastest.
Arguments:
- state_field: float32 [6, 256, 515], P('group', 'circ'), parts along dimension 0, may hold values from -3 to 3
- direction: float32 [6, 256, 515], P('group', 'circ'), parts along dimension 0, may hold values from -6 to 6
- skin_thickness: float32 [256, 515], P('circ'), may hold values from 0.2 to 3
- stringer_column: int32 [16], P('circ'), may hold values from 0 to 253, as said below
Outputs:
- lanczos_vectors: float32 [6, 3, 256, 515], P('group', None, 'circ'), parts along dimension 0
- lanczos_diagonal: float32 [6], P('group'), parts along dimension 0
- lanczos_subdiagonal: float32 [6], P('group'), parts along dimension 0
There are 2 independent parts, one for each index of `group`. A program takes and returns all parts, laid end to end along the dimension named above; an argument that names none is the same for every part. Nothing has to cross between parts.
Inputs may be any that keep to these rules, and one draw needn't show every extreme that they name: `stringer_column`: stringer k is attached at the start of span c with k * 16 <= c <= (k + 1) * 16 - 3.
All inputs are finite; a program needn't handle non-finite values.
Results may differ from a plain program's by a relative error of at most 0.0003.
Values sent between devices are 32-bit elements; how exact they have to be, the bound alone decides.
No kernel may reach another device: no remote copies, remote signals or barrier semaphores. Data moves between devices by JAX's collectives and lax.ppermute only.
A program may use at most 64 MiB of HBM per device.

v0:
```python
import math

import jax
import jax.numpy as jnp
from jax import lax
from jax.sharding import PartitionSpec as P

STEPS = 3


POISSON = 0.3
EPSILON = 1e-06
STRINGER_AXIAL = 40.0
STRINGER_BENDING = 20.0
END_STIFF = 4.0


def with_halo(cells, sides, width):
    for axis, dim in sides:
        count = lax.axis_size(axis)
        head = lax.slice_in_dim(cells, 0, width, axis=dim)
        tail = lax.slice_in_dim(cells, cells.shape[dim] - width, cells.shape[dim], axis=dim)
        cells = jnp.concatenate(
            [
                lax.ppermute(tail, axis, [(i, (i + 1) % count) for i in range(count)]),
                cells,
                lax.ppermute(head, axis, [((i + 1) % count, i) for i in range(count)]),
            ],
            axis=dim,
        )
    return cells


def gauss_rule():
    inner_root = math.sqrt(3.0 / 7.0 - 2.0 / 7.0 * math.sqrt(6.0 / 5.0))
    outer_root = math.sqrt(3.0 / 7.0 + 2.0 / 7.0 * math.sqrt(6.0 / 5.0))
    weight_inner = (18.0 + math.sqrt(30.0)) / 72.0
    weight_outer = (18.0 - math.sqrt(30.0)) / 72.0
    points = [
        0.5 - 0.5 * outer_root,
        0.5 - 0.5 * inner_root,
        0.5 + 0.5 * inner_root,
        0.5 + 0.5 * outer_root,
    ]
    weights = [weight_outer, weight_inner, weight_inner, weight_outer]
    return (points, weights)


def basis_value(degree, offset, location):
    other_side = 1.0 - location
    if degree == 0:
        values = [
            other_side**3 / 6.0,
            (3.0 * location**3 - 6.0 * location**2 + 4.0) / 6.0,
            (-3.0 * location**3 + 3.0 * location**2 + 3.0 * location + 1.0) / 6.0,
            location**3 / 6.0,
        ]
    elif degree == 1:
        values = [
            -(other_side**2) / 2.0,
            1.5 * location**2 - 2.0 * location,
            -1.5 * location**2 + location + 0.5,
            location**2 / 2.0,
        ]
    else:
        values = [other_side, 3.0 * location - 2.0, 1.0 - 3.0 * location, location]
    return values[offset]


def spline_table():
    points, weights = gauss_rule()
    spline_rows = []
    for degree in range(3):
        row_list = []
        for offset in range(4):
            row_list.append([basis_value(degree, offset, location) for location in points])
        spline_rows.append(row_list)
    return (spline_rows, weights)


def axial_take(values, degree, axial_point, spline_rows):
    elements = values.shape[-1] - 3
    summed = spline_rows[degree][0][axial_point] * values[..., 0:elements]
    for offset in range(1, 4):
        summed = (
            summed
            + spline_rows[degree][offset][axial_point] * values[..., offset : offset + elements]
        )
    return summed


def axial_put(values, degree, axial_point, spline_rows, weight):
    summed = 0.0
    for offset in range(4):
        pad_widths = [(0, 0)] * (values.ndim - 1) + [(offset, 3 - offset)]
        summed = summed + jnp.pad(
            spline_rows[degree][offset][axial_point] * weight * values, pad_widths
        )
    return summed


def circ_take(values, degree, circ_point, spline_rows):
    spans = values.shape[-2] - 3
    summed = spline_rows[degree][0][circ_point] * values[..., 0:spans, :]
    for offset in range(1, 4):
        summed = (
            summed
            + spline_rows[degree][offset][circ_point] * values[..., offset : offset + spans, :]
        )
    return summed


def circ_put(term_pairs, circ_point, spline_rows, weight):
    summed = 0.0
    for offset in range(4):
        combined = 0.0
        for degree, values in term_pairs:
            combined = combined + spline_rows[degree][offset][circ_point] * values
        pad_widths = [(0, 0)] * (combined.ndim - 2) + [(offset, 3 - offset), (0, 0)]
        summed = summed + jnp.pad(weight * combined, pad_widths)
    return summed


def membrane_forces(strain_axial, strain_circ, strain_shear, stiffness):
    return (
        stiffness * (strain_axial + POISSON * strain_circ),
        stiffness * (POISSON * strain_axial + strain_circ),
        stiffness * 0.5 * (1.0 - POISSON) * strain_shear,
    )


def state_point(state_zero, state_one, thick_zero, circ_point, spline_rows, radius):
    axial_along = circ_take(state_one[0], 0, circ_point, spline_rows)
    axial_across = circ_take(state_zero[0], 1, circ_point, spline_rows)
    circ_across = circ_take(state_zero[1], 1, circ_point, spline_rows)
    circ_along = circ_take(state_one[1], 0, circ_point, spline_rows)
    deflect = circ_take(state_zero[2], 0, circ_point, spline_rows)
    deflect_along = circ_take(state_one[2], 0, circ_point, spline_rows)
    deflect_across = circ_take(state_zero[2], 1, circ_point, spline_rows)
    thickness = circ_take(thick_zero, 0, circ_point, spline_rows)
    inverse = 1.0 / (1.0 - POISSON * POISSON)
    membrane = inverse * thickness
    bending = inverse * thickness**3 / 12.0
    strain_axial = axial_along + 0.5 * deflect_along**2
    strain_circ = circ_across + deflect / radius + 0.5 * deflect_across**2
    strain_shear = axial_across + circ_along + deflect_along * deflect_across
    forces = membrane_forces(strain_axial, strain_circ, strain_shear, membrane)
    return (deflect_along, deflect_across) + forces + (membrane, bending)


def point_pairs(state_set, vector_zero, vector_one, vector_two, circ_point, spline_rows, radius):
    deflect_along, deflect_across, force_axial, force_circ, force_shear, membrane, bending = (
        state_set
    )
    delta_axial_along = circ_take(vector_one[0], 0, circ_point, spline_rows)
    delta_axial_across = circ_take(vector_zero[0], 1, circ_point, spline_rows)
    delta_circ_across = circ_take(vector_zero[1], 1, circ_point, spline_rows)
    delta_circ_along = circ_take(vector_one[1], 0, circ_point, spline_rows)
    delta_deflect = circ_take(vector_zero[2], 0, circ_point, spline_rows)
    delta_slope_along = circ_take(vector_one[2], 0, circ_point, spline_rows)
    delta_slope_across = circ_take(vector_zero[2], 1, circ_point, spline_rows)
    delta_curve_along = circ_take(vector_two, 0, circ_point, spline_rows)
    delta_curve_across = circ_take(vector_zero[2], 2, circ_point, spline_rows)
    delta_twist = circ_take(vector_one[2], 1, circ_point, spline_rows)
    strain_axial = delta_axial_along + deflect_along * delta_slope_along
    strain_circ = delta_circ_across + delta_deflect / radius + deflect_across * delta_slope_across
    strain_shear = (
        delta_axial_across
        + delta_circ_along
        + deflect_along * delta_slope_across
        + deflect_across * delta_slope_along
    )
    axial_force, circ_force, shear_force = membrane_forces(
        strain_axial, strain_circ, strain_shear, membrane
    )
    axial_moment, circ_moment, twist_moment = membrane_forces(
        -delta_curve_along, -delta_curve_across, -2.0 * delta_twist, bending
    )
    slope_along = (
        axial_force * deflect_along
        + shear_force * deflect_across
        + force_axial * delta_slope_along
        + force_shear * delta_slope_across
    )
    slope_across = (
        circ_force * deflect_across
        + shear_force * deflect_along
        + force_circ * delta_slope_across
        + force_shear * delta_slope_along
    )
    return {
        (0, 1): [(0, axial_force)],
        (0, 0): [(1, shear_force)],
        (1, 0): [(1, circ_force)],
        (1, 1): [(0, shear_force)],
        (2, 0): [(0, circ_force / radius), (1, slope_across), (2, -circ_moment)],
        (2, 1): [(0, slope_along), (1, -2.0 * twist_moment)],
        (2, 2): [(0, -axial_moment)],
    }


def prepare_state(state_ext, thick_ext, radius, spline_rows):
    state_table = []
    for axial_point in range(4):
        state_zero = axial_take(state_ext, 0, axial_point, spline_rows)
        state_one = axial_take(state_ext, 1, axial_point, spline_rows)
        thick_zero = axial_take(thick_ext, 0, axial_point, spline_rows)
        state_table.append(
            [
                state_point(state_zero, state_one, thick_zero, circ_point, spline_rows, radius)
                for circ_point in range(4)
            ]
        )
    return state_table


def skin_product(state_points, vector_field, radius, spline_rows, weights):
    comp_totals = [0.0, 0.0, 0.0]
    for axial_point in range(4):
        vector_zero = axial_take(vector_field, 0, axial_point, spline_rows)
        vector_one = axial_take(vector_field, 1, axial_point, spline_rows)
        vector_two = axial_take(vector_field[2], 2, axial_point, spline_rows)
        holders = {}
        for circ_point in range(4):
            pair_map = point_pairs(
                state_points[axial_point][circ_point],
                vector_zero,
                vector_one,
                vector_two,
                circ_point,
                spline_rows,
                radius,
            )
            for slot_pair in sorted(pair_map):
                added = circ_put(pair_map[slot_pair], circ_point, spline_rows, weights[circ_point])
                holders[slot_pair] = holders[slot_pair] + added if slot_pair in holders else added
        for slot_pair in sorted(holders):
            component = slot_pair[0]
            comp_totals[component] = comp_totals[component] + axial_put(
                holders[slot_pair], slot_pair[1], axial_point, spline_rows, weights[axial_point]
            )
    return jnp.stack(comp_totals)


def placement_matrix(attach, columns):
    offset_diff = columns[None, :] - attach[:, None]
    return (
        jnp.where(offset_diff == 0, 1.0 / 6.0, 0.0)
        + jnp.where(offset_diff == 1, 4.0 / 6.0, 0.0)
        + jnp.where(offset_diff == 2, 1.0 / 6.0, 0.0)
    ).astype(jnp.float32)


def stringer_state(state_field, placement, spline_rows):
    line_fields = jnp.einsum(
        "kc,ica->ika",
        placement,
        jnp.stack([state_field[0], state_field[2]]),
        precision=lax.Precision.HIGHEST,
    )
    return [
        (
            axial_take(line_fields[0], 1, axial_point, spline_rows),
            axial_take(line_fields[1], 1, axial_point, spline_rows),
        )
        for axial_point in range(4)
    ]


def stringer_product(stringer_points, vector_field, placement, spline_rows, weights):
    delta_lines = jnp.einsum(
        "kc,ica->ika",
        placement,
        jnp.stack([vector_field[0], vector_field[2]]),
        precision=lax.Precision.HIGHEST,
    )
    axial_total = 0.0
    deflect_total = 0.0
    for axial_point in range(4):
        line_along, line_slope = stringer_points[axial_point]
        delta_along = axial_take(delta_lines[0], 1, axial_point, spline_rows)
        delta_slope = axial_take(delta_lines[1], 1, axial_point, spline_rows)
        delta_curve = axial_take(delta_lines[1], 2, axial_point, spline_rows)
        stretch = line_along + 0.5 * line_slope**2
        delta_stretch = delta_along + line_slope * delta_slope
        weight = weights[axial_point]
        axial_total = axial_total + axial_put(
            STRINGER_AXIAL * delta_stretch, 1, axial_point, spline_rows, weight
        )
        deflect_total = (
            deflect_total
            + axial_put(
                STRINGER_AXIAL * (delta_stretch * line_slope + stretch * delta_slope),
                1,
                axial_point,
                spline_rows,
                weight,
            )
            + axial_put(STRINGER_BENDING * delta_curve, 2, axial_point, spline_rows, weight)
        )
    spread_back = jnp.einsum(
        "kc,ika->ica",
        placement,
        jnp.stack([axial_total, deflect_total]),
        precision=lax.Precision.HIGHEST,
    )
    return jnp.stack([spread_back[0], jnp.zeros_like(spread_back[0]), spread_back[1]])


def end_product(vector_field):
    kernel = jnp.array([1.0, 4.0, 1.0], jnp.float32) / 6.0
    first_row = (
        END_STIFF * (vector_field[..., 0] + 4.0 * vector_field[..., 1] + vector_field[..., 2]) / 6.0
    )
    last_row = (
        END_STIFF
        * (vector_field[..., -3] + 4.0 * vector_field[..., -2] + vector_field[..., -1])
        / 6.0
    )
    length = vector_field.shape[-1]
    pad_lead = [(0, 0)] * (vector_field.ndim - 1)
    return jnp.pad(first_row[..., None] * kernel, pad_lead + [(0, length - 3)]) + jnp.pad(
        last_row[..., None] * kernel, pad_lead + [(length - 3, 0)]
    )


def per_device(state_field, direction, skin_thickness, stringer_column):
    cycle_size = lax.axis_size("circ")
    own_cols = state_field.shape[1]
    axial_count = state_field.shape[2]
    count_all = 3.0 * own_cols * axial_count * cycle_size
    radius = own_cols * cycle_size / (2.0 * math.pi)
    spline_rows, weights = spline_table()
    local_attach = stringer_column - lax.axis_index("circ") * own_cols
    placement = placement_matrix(local_attach, jnp.arange(own_cols, dtype=jnp.int32))
    stringer_points = stringer_state(state_field, placement, spline_rows)
    packed = jnp.concatenate([state_field, skin_thickness[None]], axis=0)
    packed_ext = with_halo(packed, (("circ", 1),), 3)
    state_points = prepare_state(packed_ext[:3], packed_ext[3], radius, spline_rows)

    def apply_operator(vector_own):
        vector_ext = with_halo(vector_own, (("circ", 1),), 3)
        skin_full = skin_product(state_points, vector_ext, radius, spline_rows, weights)
        skin_own = skin_full[:, 3 : 3 + own_cols]
        return (
            skin_own
            + stringer_product(stringer_points, vector_own, placement, spline_rows, weights)
            + end_product(vector_own)
        )

    def joined_step(carry, unused):
        raw_vector, previous = carry
        image_raw = apply_operator(raw_vector)
        norm_square, cross_term = lax.psum(
            (jnp.sum(raw_vector * raw_vector), jnp.sum(raw_vector * image_raw)), "circ"
        )
        beta_prev = jnp.sqrt(norm_square / count_all + EPSILON)
        current = raw_vector / beta_prev
        alpha_value = cross_term / (count_all * beta_prev * beta_prev)
        next_raw = image_raw / beta_prev - alpha_value * current - beta_prev * previous
        return ((next_raw, current), (current, alpha_value, beta_prev))

    start = (direction, jnp.zeros_like(direction))
    final_carry, stacked = lax.scan(joined_step, start, None, length=STEPS)
    raw_vector = final_carry[0]
    final_square = lax.psum(jnp.sum(raw_vector * raw_vector), "circ")
    beta_final = jnp.sqrt(final_square / count_all + EPSILON)
    vectors_all = jnp.concatenate([stacked[0][1:], (raw_vector / beta_final)[None]], axis=0)
    betas_all = jnp.concatenate([stacked[2][1:], beta_final[None]], axis=0)
    return (vectors_all, stacked[1], betas_all)


def solution(mesh):
    in_specs = (P("group", "circ", None), P("group", "circ", None), P("circ", None), P("circ"))
    out_specs = (P("group", None, "circ", None), P("group"), P("group"))
    return jax.shard_map(
        per_device, mesh=mesh, in_specs=in_specs, out_specs=out_specs, check_vma=False
    )
```

profile of v0, /device:TPU:0, one launch (start us, length us, event | category | flops | bytes accessed | tf_op | source)
XLA Modules:
  0.0 325.9 jit_solution(6232991862057950079)
XLA Ops:
  0.7 0.9 copy.57
  2.2 5.0 %collective-permute-start.3 = (f32[4,3,515]{2,1,0:T(4,128)S(1)}, f32[4,3,515]{2,1,0:T(4,128)S(1)}, u32[]{:S(2)}, u32[]{:S(2)}) collective-permute-start(f32[4,3,515]{2,1,0:T(4,128)S(1)} %get-tuple-element.5667), channel_id=1, source_target_pairs={{1,0},{2,1},{3,2},{4,3},{5,4},{6,5},{7,6},{8,7},{9,8},{10,9},{11,1... | collective-permute-start | bytes 74168 | tf_op jit(solution)/shard_map/ppermute | solution.py:27
  10.5 0.8 add_multiply_fusion.163
  11.3 0.8 add_multiply_fusion.162
  12.0 0.8 add_multiply_fusion.161
  12.8 0.8 add_multiply_fusion.160
  13.5 0.8 add_multiply_fusion.171
  14.3 0.8 add_multiply_fusion.170
  15.0 0.8 add_multiply_fusion.169
  15.8 0.8 add_multiply_fusion.168
  16.8 0.8 add_multiply_fusion.179
  17.5 0.8 add_multiply_fusion.178
  18.3 0.8 add_multiply_fusion.177
  19.1 0.8 add_multiply_fusion.176
  19.8 0.8 add_multiply_fusion.187
  20.6 0.8 add_multiply_fusion.186
  21.3 0.8 add_multiply_fusion.185
  22.1 0.8 add_multiply_fusion.184
  34.8 257.5 %while.23 = (s32[]{:T(128)}, f32[3,16,515]{2,1,0:T(8,128)S(1)}, f32[3,16,515]{2,1,0:T(8,128)S(1)}, f32[3,3,16,515]{3,2,1,0:T(8,128)}, f32[3]{0:T(128)}, /*index=...) while((s32[]{:T(128)}, f32[3,16,515]{2,1,0:T(8,128)S(1)}, ...), condition=%wide.region_5.6_spmd.clone.clone, body=%wide.region_0.5_spmd.sunk.clone.clone.sunk | while | flops 37853512 | bytes 117284328 | solution.py:364
  35.4 3.2 collective-permute-start
  42.8 1.8 collective-permute-done.1
  47.5 0.7 copy-done.25
  51.3 0.7 copy-done.19
  55.4 0.7 copy-done.44
  58.4 0.7 copy-done.21
  61.6 0.8 copy-done.58
  65.2 0.7 copy-done.11
  67.4 0.8 copy-done.37
  69.4 0.7 copy-done.36
  72.4 0.7 copy-done.13
  74.2 0.7 copy-done.15
  79.4 0.8 copy-done.55
  82.6 0.8 multiply_reduce_fusion.10
  83.4 32.8 %all-reduce.612 = (f32[]{:T(128)}, f32[]{:T(128)}) all-reduce(f32[]{:T(128)} %get-tuple-element.8618, f32[]{:T(128)} %multiply_reduce_fusion.10), channel_id=1, replica_groups=mesh['group'=2,'circ'=16] {'circ'}, use_global_device_ids=true, to_apply=%region_2.2 | all-reduce | flops 2 | bytes 16 | tf_op jit(solution)/shard_map/while/body/eval_jaxpr/psum | solution.py:354
  118.1 1.5 multiply_reduce_fusion.11
  128.1 1.3 collective-permute-done.1
  132.2 0.7 copy-done.25
  136.1 0.7 copy-done.19
  143.2 0.7 copy-done.21
  146.4 0.8 copy-done.58
  150.0 0.7 copy-done.11
  152.1 0.8 copy-done.37
  154.1 0.7 copy-done.36
  157.2 0.7 copy-done.13
  158.9 0.7 copy-done.15
  164.2 0.8 copy-done.55
  167.4 0.8 multiply_reduce_fusion.10
  168.2 32.8 %all-reduce.612 = (f32[]{:T(128)}, f32[]{:T(128)}) all-reduce(f32[]{:T(128)} %get-tuple-element.8618, f32[]{:T(128)} %multiply_reduce_fusion.10), channel_id=1, replica_groups=mesh['group'=2,'circ'=16] {'circ'}, use_global_device_ids=true, to_apply=%region_2.2 | all-reduce | flops 2 | bytes 16 | tf_op jit(solution)/shard_map/while/body/eval_jaxpr/psum | solution.py:354
  202.9 1.5 multiply_reduce_fusion.11
  212.9 1.3 collective-permute-done.1
  217.0 0.7 copy-done.25
  220.8 0.7 copy-done.19
  227.9 0.7 copy-done.21
  231.1 0.8 copy-done.58
  234.7 0.7 copy-done.11
  236.9 0.8 copy-done.37
  241.9 0.7 copy-done.13
  243.7 0.7 copy-done.15
  248.9 0.8 copy-done.55
  252.2 0.8 multiply_reduce_fusion.10
  252.9 32.8 %all-reduce.612 = (f32[]{:T(128)}, f32[]{:T(128)}) all-reduce(f32[]{:T(128)} %get-tuple-element.8618, f32[]{:T(128)} %multiply_reduce_fusion.10), channel_id=1, replica_groups=mesh['group'=2,'circ'=16] {'circ'}, use_global_device_ids=true, to_apply=%region_2.2 | all-reduce | flops 2 | bytes 16 | tf_op jit(solution)/shard_map/while/body/eval_jaxpr/psum | solution.py:354
  287.7 1.5 multiply_reduce_fusion.11
  293.0 30.1 %psum.29 = f32[]{:T(128)} all-reduce(f32[]{:T(128)} %multiply_reduce_fusion.5), channel_id=1, replica_groups=mesh['group'=2,'circ'=16] {'circ'}, use_global_device_ids=true, to_apply=%region_7.8 | all-reduce | flops 1 | bytes 8 | tf_op jit(solution)/shard_map/psum | solution.py:366
  325.1 0.8 pad_maximum_fusion.4
  (1066 shorter events, 130.3 us)
Async XLA Ops:
  0.6 1.0 copy-start.60
  0.6 1.0 copy-start.62
  1.6 8.5 %collective-permute-start.2 = (f32[4,3,515]{2,1,0:T(4,128)S(1)}, f32[4,3,515]{2,1,0:T(4,128)S(1)}, u32[]{:S(2)}, u32[]{:S(2)}) collective-permute-start(f32[4,3,515]{2,1,0:T(4,128)S(1)} %get-tuple-element.5666), channel_id=1, source_target_pairs={{0,1},{1,2},{2,3},{3,4},{4,5},{5,6},{6,7},{7,8},{8,9},{9,10},{10,1... | collective-permute-start | bytes 74168 | tf_op jit(solution)/shard_map/ppermute | solution.py:25
  2.2 7.9 %collective-permute-start.3 = (f32[4,3,515]{2,1,0:T(4,128)S(1)}, f32[4,3,515]{2,1,0:T(4,128)S(1)}, u32[]{:S(2)}, u32[]{:S(2)}) collective-permute-start(f32[4,3,515]{2,1,0:T(4,128)S(1)} %get-tuple-element.5667), channel_id=1, source_target_pairs={{1,0},{2,1},{3,2},{4,3},{5,4},{6,5},{7,6},{8,7},{9,8},{10,9},{11,1... | collective-permute-start | bytes 74168 | tf_op jit(solution)/shard_map/ppermute | solution.py:27
  15.8 11.2 %copy-start = (f32[19,512]{1,0:T(8,128)}, f32[19,512]{1,0:T(8,128)S(1)}, u32[]{:S(2)}) copy-start(f32[19,512]{1,0:T(8,128)S(1)} %get-tuple-element.8385) | copy-start | bytes 116740
  15.8 11.2 %copy-start.2 = (f32[19,512]{1,0:T(8,128)}, f32[19,512]{1,0:T(8,128)S(1)}, u32[]{:S(2)}) copy-start(f32[19,512]{1,0:T(8,128)S(1)} %get-tuple-element.8384) | copy-start | bytes 116740
  16.6 11.1 %copy-start.4 = (f32[19,512]{1,0:T(8,128)}, f32[19,512]{1,0:T(8,128)S(1)}, u32[]{:S(2)}) copy-start(f32[19,512]{1,0:T(8,128)S(1)} %get-tuple-element.8388) | copy-start | bytes 116740
  16.6 11.1 %copy-start.6 = (f32[19,512]{1,0:T(8,128)}, f32[19,512]{1,0:T(8,128)S(1)}, u32[]{:S(2)}) copy-start(f32[19,512]{1,0:T(8,128)S(1)} %get-tuple-element.8387) | copy-start | bytes 116740
  33.3 0.8 copy-start.7
  34.0 0.8 copy-start.3
  35.4 7.4 %collective-permute-start = (f32[3,3,515]{2,1,0:T(4,128)}, f32[3,3,515]{2,1,0:T(4,128)S(1)}, u32[]{:S(2)}, u32[]{:S(2)}) collective-permute-start(f32[3,3,515]{2,1,0:T(4,128)} %get-tuple-element.7516), channel_id=1, source_target_pairs={{1,0},{2,1},{3,2},{4,3},{5,4},{6,5},{7,6},{8,7},{9,8},{10,9},{11,1... | collective-permute-start | bytes 55628 | tf_op jit(solution)/shard_map/while/body/eval_jaxpr/ppermute | solution.py:27
  38.7 6.0 %collective-permute-start.1 = (f32[3,3,515]{2,1,0:T(4,128)S(1)}, f32[3,3,515]{2,1,0:T(4,128)S(1)}, u32[]{:S(2)}, u32[]{:S(2)}) collective-permute-start(f32[3,3,515]{2,1,0:T(4,128)S(1)} %get-tuple-element.7517), channel_id=1, source_target_pairs={{0,1},{1,2},{2,3},{3,4},{4,5},{5,6},{6,7},{7,8},{8,9},{9,10},{10,1... | collective-permute-start | bytes 55628 | tf_op jit(solution)/shard_map/while/body/eval_jaxpr/ppermute | solution.py:25
  42.8 39.7 %copy-start.70 = (f32[3]{0:T(128)}, f32[3]{0:T(128)S(1)}, u32[]{:S(2)}) copy-start(f32[3]{0:T(128)S(1)} %pad.6115.clone.2) | copy-start | bytes 40 | tf_op jit(solution)/shard_map/while
  45.7 0.8 copy-start.10
  45.7 0.8 copy-start.50
  47.4 0.8 copy-start.26
  47.4 0.8 copy-start.51
  49.5 0.8 copy-start.46
  51.3 0.8 copy-start.47
  58.4 0.8 copy-start.48
  60.2 0.8 copy-start.24
  60.2 0.8 copy-start.49
  65.2 0.8 copy-start.12
  65.2 0.8 copy-start.39
  72.4 0.8 copy-start.14
  72.4 0.8 copy-start.40
  74.1 0.8 copy-start.41
  78.1 0.8 copy-start.43
  123.4 4.7 %collective-permute-start = (f32[3,3,515]{2,1,0:T(4,128)}, f32[3,3,515]{2,1,0:T(4,128)S(1)}, u32[]{:S(2)}, u32[]{:S(2)}) collective-permute-start(f32[3,3,515]{2,1,0:T(4,128)} %get-tuple-element.7516), channel_id=1, source_target_pairs={{1,0},{2,1},{3,2},{4,3},{5,4},{6,5},{7,6},{8,7},{9,8},{10,9},{11,1... | collective-permute-start | bytes 55628 | tf_op jit(solution)/shard_map/while/body/eval_jaxpr/ppermute | solution.py:27
  123.4 6.0 %collective-permute-start.1 = (f32[3,3,515]{2,1,0:T(4,128)S(1)}, f32[3,3,515]{2,1,0:T(4,128)S(1)}, u32[]{:S(2)}, u32[]{:S(2)}) collective-permute-start(f32[3,3,515]{2,1,0:T(4,128)S(1)} %get-tuple-element.7517), channel_id=1, source_target_pairs={{0,1},{1,2},{2,3},{3,4},{4,5},{5,6},{6,7},{7,8},{8,9},{9,10},{10,1... | collective-permute-start | bytes 55628 | tf_op jit(solution)/shard_map/while/body/eval_jaxpr/ppermute | solution.py:25
  128.1 39.2 %copy-start.70 = (f32[3]{0:T(128)}, f32[3]{0:T(128)S(1)}, u32[]{:S(2)}) copy-start(f32[3]{0:T(128)S(1)} %pad.6115.clone.2) | copy-start | bytes 40 | tf_op jit(solution)/shard_map/while
  130.4 0.8 copy-start.10
  130.4 0.8 copy-start.50
  132.2 0.8 copy-start.51
  136.0 0.8 copy-start.20
  136.0 0.8 copy-start.47
  143.1 0.8 copy-start.22
  143.2 0.8 copy-start.48
  145.0 0.8 copy-start.49
  149.9 0.8 copy-start.12
  149.9 0.8 copy-start.39
  157.1 0.8 copy-start.40
  158.9 0.8 copy-start.16
  158.9 0.8 copy-start.41
  162.8 0.8 copy-start.18
  162.8 0.8 copy-start.43
  208.2 4.7 %collective-permute-start = (f32[3,3,515]{2,1,0:T(4,128)}, f32[3,3,515]{2,1,0:T(4,128)S(1)}, u32[]{:S(2)}, u32[]{:S(2)}) collective-permute-start(f32[3,3,515]{2,1,0:T(4,128)} %get-tuple-element.7516), channel_id=1, source_target_pairs={{1,0},{2,1},{3,2},{4,3},{5,4},{6,5},{7,6},{8,7},{9,8},{10,9},{11,1... | collective-permute-start | bytes 55628 | tf_op jit(solution)/shard_map/while/body/eval_jaxpr/ppermute | solution.py:27
  208.2 6.0 %collective-permute-start.1 = (f32[3,3,515]{2,1,0:T(4,128)S(1)}, f32[3,3,515]{2,1,0:T(4,128)S(1)}, u32[]{:S(2)}, u32[]{:S(2)}) collective-permute-start(f32[3,3,515]{2,1,0:T(4,128)S(1)} %get-tuple-element.7517), channel_id=1, source_target_pairs={{0,1},{1,2},{2,3},{3,4},{4,5},{5,6},{6,7},{7,8},{8,9},{9,10},{10,1... | collective-permute-start | bytes 55628 | tf_op jit(solution)/shard_map/while/body/eval_jaxpr/ppermute | solution.py:25
  212.9 39.2 %copy-start.70 = (f32[3]{0:T(128)}, f32[3]{0:T(128)S(1)}, u32[]{:S(2)}) copy-start(f32[3]{0:T(128)S(1)} %pad.6115.clone.2) | copy-start | bytes 40 | tf_op jit(solution)/shard_map/while
  215.2 0.8 copy-start.10
  215.2 0.8 copy-start.50
  216.9 0.8 copy-start.26
  216.9 0.8 copy-start.51
  219.0 0.8 copy-start.46
  220.8 0.8 copy-start.20
  220.8 0.8 copy-start.47
  227.9 0.8 copy-start.48
  229.8 0.8 copy-start.49
  234.7 0.8 copy-start.12
  234.7 0.8 copy-start.39
  241.9 0.8 copy-start.40
  243.7 0.8 copy-start.41
  247.6 0.8 copy-start.43
  292.3 32.1 %copy-start.61 = (f32[3,3,16,515]{3,2,1,0:T(8,128)S(1)}, f32[3,3,16,515]{3,2,1,0:T(8,128)}, u32[]{:S(2)}) copy-start(f32[3,3,16,515]{3,2,1,0:T(8,128)} %get-tuple-element.2664) | copy-start | bytes 889924
  (153 other events, 116.2 us)
where the time goes:
time: 332 us; the launch traced here: 326 us
  blocking collectives  128 us (39%)
  local copies, waits for them, and re-layouts  92.6 us (28%)
  other arithmetic  78.5 us (24%)
  starting transfers between devices  9.86 us (3%)
  loops' own time  9.1 us (3%)
  waiting for transfers between devices  4.53 us (1%)
    psum x3, blocking collectives, joined_step(): lax.psum((jnp.sum(raw_vector * raw_vector), jnp.sum(raw_vector * image_ra...  98.3 us
    while x399, local copies, waits for them, and re-layouts  85.4 us
    psum x1, blocking collectives, per_device(): final_square = lax.psum(jnp.sum(raw_vector * raw_vector), 'circ')  30.1 us
    mul x354, other arithmetic, circ_put(): summed = summed + jnp.pad(weight * combined, pad_widths)  23.2 us
    mul x16, other arithmetic, membrane_forces(): stiffness * (strain_axial + POISSON * strain_circ)  12.1 us
    div x16, other arithmetic, state_point(): bending = inverse * thickness ** 3 / 12.0  11.1 us
    mul x201, other arithmetic, axial_put(): spline_rows[degree][offset][axial_point] * weight * values  10.4 us
    another operation x1, loops' own time, per_device(): final_carry, stacked = lax.scan(joined_step, start, None, length=STEPS)  9.1 us
  transfers between devices with their start and end apart: 8, of which 3 were waited for; matrix products, arithmetic and copies ran while one was open for 2% of the time, Pallas kernels for 0%

commit v1 on v0

v1 whole, which is shorter than its diff:
```python
import functools
import math

import jax
import jax.numpy as jnp
from jax import lax
from jax.experimental import pallas as pl
from jax.experimental.pallas import tpu as pltpu
from jax.sharding import PartitionSpec as P

STEPS = 3

POISSON = 0.3
EPSILON = 1e-06
STRINGER_AXIAL = 40.0
STRINGER_BENDING = 20.0
END_STIFF = 4.0

LANES = 128
SUBS = 8
HALF = 4
HALO = 3 * STEPS

A1, B1, C0, C1, C2, DA0, DB0, DC0, DC1, DDC0, H0 = range(11)
F01, F00, F10, F11, F20, F20Q, F20L, F21, F21Q, F22 = range(10)
S_WX, S_WS, S_NX, S_NS, S_NG, S_A, S_AG, S_D = range(8)


def gauss_rule():
    inner_root = math.sqrt(3.0 / 7.0 - 2.0 / 7.0 * math.sqrt(6.0 / 5.0))
    outer_root = math.sqrt(3.0 / 7.0 + 2.0 / 7.0 * math.sqrt(6.0 / 5.0))
    weight_inner = (18.0 + math.sqrt(30.0)) / 72.0
    weight_outer = (18.0 - math.sqrt(30.0)) / 72.0
    points = [
        0.5 - 0.5 * outer_root,
        0.5 - 0.5 * inner_root,
        0.5 + 0.5 * inner_root,
        0.5 + 0.5 * outer_root,
    ]
    return points, [weight_outer, weight_inner, weight_inner, weight_outer]


def cubic(t):
    s = 1.0 - t
    return [
        s**3 / 6.0,
        (3.0 * t**3 - 6.0 * t**2 + 4.0) / 6.0,
        (-3.0 * t**3 + 3.0 * t**2 + 3.0 * t + 1.0) / 6.0,
        t**3 / 6.0,
    ]


def quadratic(t):
    return [(1.0 - t) ** 2 / 2.0, -(t**2) + t + 0.5, t**2 / 2.0]


POINTS, WEIGHTS = gauss_rule()


def take4(z):
    p03, m03, p12, m12 = z[0] + z[3], z[0] - z[3], z[1] + z[2], z[1] - z[2]

    def at(t, scale=1.0):
        b = [scale * x for x in cubic(t)]
        even = p03 * (0.5 * (b[0] + b[3])) + p12 * (0.5 * (b[1] + b[2]))
        odd = m03 * (0.5 * (b[0] - b[3])) + m12 * (0.5 * (b[1] - b[2]))
        return even, odd

    return at


def take3(d):
    p, m = d[0] + d[2], d[0] - d[2]

    def at(t, scale=1.0):
        q = [scale * x for x in quadratic(t)]
        return p * (0.5 * (q[0] + q[2])) + d[1] * q[1], m * (0.5 * (q[0] - q[2]))

    return at


def take2(g):
    even, m = 0.5 * (g[0] + g[1]), g[0] - g[1]

    def at(t):
        return even, m * (0.5 - t)

    return at


def both(pair):
    return pair[0] + pair[1], pair[0] - pair[1]


def merged(first, second):
    return first[0] + second[0], first[1] + second[1]


def put4(pairs, scale=1.0):
    sums = None
    for t, (one, two) in pairs:
        s, d = one + two, one - two
        b = [scale * x for x in cubic(t)]
        terms = [
            s * (0.5 * (b[0] + b[3])),
            d * (0.5 * (b[0] - b[3])),
            s * (0.5 * (b[1] + b[2])),
            d * (0.5 * (b[1] - b[2])),
        ]
        sums = terms if sums is None else [x + y for x, y in zip(sums, terms)]
    e03, o03, e12, o12 = sums
    return [e03 + o03, e12 + o12, e12 - o12, e03 - o03]


def put3(pairs):
    sums = None
    for t, (one, two) in pairs:
        s, d = one + two, one - two
        q = quadratic(t)
        terms = [s * (0.5 * (q[0] + q[2])), d * (0.5 * (q[0] - q[2])), s * q[1]]
        sums = terms if sums is None else [x + y for x, y in zip(sums, terms)]
    even, odd, middle = sums
    return [even + odd, middle, even - odd]


def put2(pairs):
    even, odd = None, None
    for t, (one, two) in pairs:
        s, d = one + two, (one - two) * (0.5 - t)
        even = s if even is None else even + s
        odd = d if odd is None else odd + d
    even = 0.5 * even
    return [even + odd, even - odd]


def krylov_kernel(
    own_cols,
    pad,
    radius,
    left_ref,
    own_ref,
    right_ref,
    krylov_ref,
    gram_ref,
    field_ref,
    take_ref,
    acc_ref,
    state_ref,
    image_ref,
    table_ref,
    line_ref,
):
    sub = lax.broadcasted_iota(jnp.int32, (SUBS, LANES), 0)
    lane = lax.broadcasted_iota(jnp.int32, (SUBS, LANES), 1)
    low = sub < HALF
    zero = jnp.zeros((SUBS, LANES), jnp.float32)

    for h in range(2):
        first, second = POINTS[h], POINTS[3 - h]
        rows = (
            list(zip(cubic(first), cubic(second)))
            + list(zip(quadratic(first), quadratic(second)))
            + [(1.0 - first, 1.0 - second), (first, second)]
        )
        for i, (x, y) in enumerate(rows):
            table_ref[h, i] = jnp.where(low, jnp.float32(x), jnp.float32(y))

    field_ref[...] = jnp.zeros_like(field_ref)
    chunks = left_ref.shape[2] // LANES
    for source, offset in (
        (left_ref, pad - HALO),
        (own_ref, pad),
        (right_ref, pad + own_cols),
    ):
        for i in range(source.shape[0]):
            for c in range(chunks):
                start = (offset + i) * SUBS * SUBS + c
                field_ref[pl.ds(start, SUBS, stride=SUBS), :] = source[
                    i, :, c * LANES : (c + 1) * LANES
                ]

    def field(col, index):
        start = pl.multiple_of(col * (SUBS * SUBS) + index * SUBS, SUBS)
        return field_ref[pl.ds(start, SUBS), :]

    def shifted(v):
        following = pltpu.roll(v, SUBS - 1, 0)
        shifts = [v] + [
            pltpu.roll(jnp.where(lane < o, following, v), LANES - o, 1) for o in range(1, 4)
        ]
        return [jnp.where(low, z, pltpu.roll(z, HALF, 0)) for z in shifts]

    def value(z, h):
        return sum(table_ref[h, o] * z[o] for o in range(4))

    def slope(d, h):
        return sum(table_ref[h, 4 + o] * d[o] for o in range(3))

    def curve(g, h):
        return table_ref[h, 7] * g[0] + table_ref[h, 8] * g[1]

    def differences(z):
        return [z[o + 1] - z[o] for o in range(len(z) - 1)]

    def axial_take(col, load, carried, thick=None):
        za, zb, zc = (shifted(load(col, i)) for i in range(3))
        da, db, dc = differences(za), differences(zb), differences(zc)
        gc = differences(dc)
        out = []
        for h in range(2):
            old_a0, old_b0, old_c0, old_c1, old_dc0 = carried[h]
            a0, b0, c0, c1 = value(za, h), value(zb, h), value(zc, h), slope(dc, h)
            take_ref[A1, col, h] = slope(da, h)
            take_ref[B1, col, h] = slope(db, h)
            take_ref[C0, col, h] = c0
            take_ref[C1, col, h] = c1
            take_ref[C2, col, h] = curve(gc, h)
            take_ref[DA0, col - 1, h] = a0 - old_a0
            take_ref[DB0, col - 1, h] = b0 - old_b0
            dc0 = c0 - old_c0
            take_ref[DC0, col - 1, h] = dc0
            take_ref[DC1, col - 1, h] = c1 - old_c1
            take_ref[DDC0, col - 2, h] = dc0 - old_dc0
            out.append((a0, b0, c0, c1, dc0))
        if thick is not None:
            zh = shifted(thick(col))
            for h in range(2):
                take_ref[H0, col, h] = value(zh, h)
        return tuple(out)

    nothing = tuple((zero,) * 5 for _ in range(2))

    def takes(name, k, h, taps):
        return [take_ref[name, k + o, h] for o in range(taps)]

    first = pad - HALO
    last = pad + own_cols - 1 + HALO - 3
    lax.fori_loop(
        first,
        last + 4,
        lambda col, carried: axial_take(
            col, field, carried, thick=lambda c: field(c, 6)
        ),
        nothing,
    )
    stringers = []
    for i, source in enumerate((left_ref, own_ref, right_ref)):
        column = jnp.max(source[0, 7:8, 0:LANES]).astype(jnp.int32)
        stringers.append(column + (pad + (i - 1) * own_cols))
    marks = (1.0 / 6.0, 4.0 / 6.0, 1.0 / 6.0)

    def line(name, column, h):
        return sum(marks[j] * take_ref[name, column + j, h] for j in range(3))

    for i, column in enumerate(stringers):
        for h in range(2):
            along, tilt = line(A1, column, h), line(C1, column, h)
            line_ref[i, h, 0] = along + 0.5 * tilt * tilt
            line_ref[i, h, 1] = tilt

    axial_weight = [WEIGHTS[0], WEIGHTS[1]]
    inverse = 1.0 / (1.0 - POISSON * POISSON)

    def prepare(k, unused):
        for h in range(2):
            u1 = take4(takes(A1, k, h, 4))
            us = take3(takes(DA0, k, h, 3))
            vs = take3(takes(DB0, k, h, 3))
            vx = take4(takes(B1, k, h, 4))
            w0 = take4(takes(C0, k, h, 4))
            w1 = take4(takes(C1, k, h, 4))
            ws = take3(takes(DC0, k, h, 3))
            h0 = take4(takes(H0, k, h, 4))
            for p in range(2):
                t = POINTS[p]
                weight = WEIGHTS[p] * axial_weight[h]
                along = both(u1(t))
                across = both(merged(vs(t), w0(t, 1.0 / radius)))
                shear = both(merged(us(t), vx(t)))
                tilt_x, tilt_s, thick = both(w1(t)), both(ws(t)), both(h0(t))
                for q in range(2):
                    wx, wc, th = tilt_x[q], tilt_s[q], thick[q]
                    ex = along[q] + 0.5 * wx * wx
                    es = across[q] + 0.5 * wc * wc
                    g = shear[q] + wx * wc
                    a = th * (inverse * weight)
                    ag = a * (0.5 * (1.0 - POISSON))
                    point = p if q == 0 else 3 - p
                    state_ref[k, h, point, S_WX] = wx
                    state_ref[k, h, point, S_WS] = wc
                    state_ref[k, h, point, S_NX] = a * (ex + POISSON * es)
                    state_ref[k, h, point, S_NS] = a * (POISSON * ex + es)
                    state_ref[k, h, point, S_NG] = ag * g
                    state_ref[k, h, point, S_A] = a
                    state_ref[k, h, point, S_AG] = ag
                    state_ref[k, h, point, S_D] = a * (th * th) * (1.0 / 12.0)
        return unused

    lax.fori_loop(first, last + 1, prepare, 0)

    def add(name, k, h, parts):
        for o, part in enumerate(parts):
            if o == len(parts) - 1:
                acc_ref[name, k + o, h] = part
            else:
                acc_ref[name, k + o, h] += part

    def span(k, unused):
        for h in range(2):
            a1 = take4(takes(A1, k, h, 4))
            b1 = take4(takes(B1, k, h, 4))
            c0 = take4(takes(C0, k, h, 4))
            c1 = take4(takes(C1, k, h, 4))
            c2 = take4(takes(C2, k, h, 4))
            as0 = take3(takes(DA0, k, h, 3))
            bs0 = take3(takes(DB0, k, h, 3))
            cs0 = take3(takes(DC0, k, h, 3))
            cx0 = take3(takes(DC1, k, h, 3))
            cc0 = take2(takes(DDC0, k, h, 2))
            parts = []
            for p in range(2):
                t = POINTS[p]
                along = both(a1(t))
                across = both(merged(bs0(t), c0(t, 1.0 / radius)))
                shear = both(merged(as0(t), b1(t)))
                tilt_x, tilt_s = both(c1(t)), both(cs0(t))
                bend_x, bend_s = both(c2(t)), both(cc0(t))
                twist = both(cx0(t, 2.0 * (1.0 - POISSON)))
                results = []
                for q in range(2):
                    point = p if q == 0 else 3 - p
                    wx, wc = state_ref[k, h, point, S_WX], state_ref[k, h, point, S_WS]
                    cx, cs = tilt_x[q], tilt_s[q]
                    ex = along[q] + wx * cx
                    es = across[q] + wc * cs
                    g = shear[q] + wx * cs + wc * cx
                    a = state_ref[k, h, point, S_A]
                    fx = a * (ex + POISSON * es)
                    fs = a * (POISSON * ex + es)
                    fg = state_ref[k, h, point, S_AG] * g
                    d = state_ref[k, h, point, S_D]
                    mx = d * (bend_x[q] + POISSON * bend_s[q])
                    ms = d * (POISSON * bend_x[q] + bend_s[q])
                    mg = d * twist[q]
                    ng = state_ref[k, h, point, S_NG]
                    sx = fx * wx + fg * wc + state_ref[k, h, point, S_NX] * cx + ng * cs
                    ss = fs * wc + fg * wx + state_ref[k, h, point, S_NS] * cs + ng * cx
                    results.append((fx, fs, fg, mx, ms, mg, sx, ss))
                parts.append((t, list(zip(*results))))

            def pick(i):
                return [(t, values[i]) for t, values in parts]

            add(F01, k, h, put4(pick(0)))
            add(F00, k, h, put3(pick(2)))
            add(F10, k, h, put3(pick(1)))
            add(F11, k, h, put4(pick(2)))
            add(F20, k, h, put4(pick(1), 1.0 / radius))
            add(F20Q, k, h, put3(pick(7)))
            add(F20L, k, h, put2(pick(4)))
            add(F21, k, h, put4(pick(6)))
            add(F21Q, k, h, put3(pick(5)))
            add(F22, k, h, put4(pick(3)))
        return unused

    def back(name, col, h):
        return acc_ref[name, col - 1, h] - acc_ref[name, col, h]

    def axial_put(zeroth, first_, second):
        t = [sum(table_ref[h, o] * zeroth[h] for h in range(2)) for o in range(4)]
        r = [sum(table_ref[h, 4 + o] * first_[h] for h in range(2)) for o in range(3)]
        t = [t[0] - r[0], t[1] + (r[0] - r[1]), t[2] + (r[1] - r[2]), t[3] + r[2]]
        if second is not None:
            l0, l1 = (sum(table_ref[h, 7 + o] * second[h] for h in range(2)) for o in range(2))
            t = [t[0] + l0, t[1] + (l1 - 2.0 * l0), t[2] + (l0 - 2.0 * l1), t[3] + l1]
        stay, cross = t[0], zero
        for o in range(1, 4):
            moved = pltpu.roll(t[o], o, 1)
            stay = stay + jnp.where(lane < o, 0.0, moved)
            cross = cross + jnp.where(lane < o, moved, 0.0)
        stay = jnp.where(low, stay + pltpu.roll(stay, HALF, 0), 0.0)
        cross = jnp.where(low, cross + pltpu.roll(cross, HALF, 0), 0.0)
        return stay + pltpu.roll(cross, 1, 0)

    ends = (sub == 0) | (sub == HALF)

    def end_part(v):
        row = (v + 4.0 * pltpu.roll(v, LANES - 1, 1) + pltpu.roll(v, LANES - 2, 1)) * (
            END_STIFF / 36.0
        )
        row = jnp.where(ends & (lane == 0), row, 0.0)
        return row + 4.0 * pltpu.roll(row, 1, 1) + pltpu.roll(row, 2, 1)

    for step in range(STEPS):
        reach = HALO - 3 * step
        first = pad - reach
        last = pad + own_cols - 1 + reach - 3

        def load(col, index, step=step):
            if step == 0:
                return field(col, 3 + index)
            return image_ref[step - 1, col, index]

        lax.fori_loop(
            first, last + 4, lambda col, carried: axial_take(col, load, carried), nothing
        )
        for name, taps in (
            (F01, 4), (F00, 3), (F10, 3), (F11, 4), (F20, 4),
            (F20Q, 3), (F20L, 2), (F21, 4), (F21Q, 3), (F22, 4),
        ):
            for o in range(taps - 1):
                for h in range(2):
                    acc_ref[name, first + o, h] = zero
        lax.fori_loop(first, last + 1, span, 0)

        for i, column in enumerate(stringers):
            for h in range(2):
                weight = jnp.float32(axial_weight[h])
                stretch, tilt = line_ref[i, h, 0], line_ref[i, h, 1]
                slope_c = line(C1, column, h)
                d_stretch = line(A1, column, h) + tilt * slope_c
                f0 = (STRINGER_AXIAL * weight) * d_stretch
                f1 = (STRINGER_AXIAL * weight) * (d_stretch * tilt + stretch * slope_c)
                f2 = (STRINGER_BENDING * weight) * line(C2, column, h)
                for j in range(3):
                    acc_ref[F01, column + j, h] += marks[j] * f0
                    acc_ref[F21, column + j, h] += marks[j] * f1
                    acc_ref[F22, column + j, h] += marks[j] * f2

        def gather(col, unused, step=step, load=load):
            halves = range(2)
            zeroth = [
                [back(F00, col, h) for h in halves],
                [back(F10, col, h) for h in halves],
                [
                    acc_ref[F20, col, h]
                    + back(F20Q, col, h)
                    + (acc_ref[F20L, col - 2, h] - acc_ref[F20L, col - 1, h])
                    - back(F20L, col, h)
                    for h in halves
                ],
            ]
            first_ = [
                [acc_ref[F01, col, h] for h in halves],
                [acc_ref[F11, col, h] for h in halves],
                [acc_ref[F21, col, h] + back(F21Q, col, h) for h in halves],
            ]
            second = [None, None, [acc_ref[F22, col, h] for h in halves]]
            for i in range(3):
                image_ref[step, col, i] = axial_put(zeroth[i], first_[i], second[i]) + end_part(
                    load(col, i)
                )
            return unused

        lax.fori_loop(first + 3, last + 1, gather, 0)

    pairs = [(i, j) for i in range(STEPS + 1) for j in range(i, STEPS + 1)]

    def inner(i, sums):
        col = pad + i
        sums = list(sums)
        for comp in range(3):
            vectors = [field(col, 3 + comp)] + [image_ref[s, col, comp] for s in range(STEPS)]
            for s, vector in enumerate(vectors):
                start = pl.multiple_of(i * (3 * SUBS) + comp * SUBS, SUBS)
                krylov_ref[s, pl.ds(start, SUBS), :] = vector
            for n, (x, y) in enumerate(pairs):
                sums[n] = sums[n] + vectors[x] * vectors[y]
        return tuple(sums)

    sums = lax.fori_loop(0, own_cols, inner, (zero,) * len(pairs))
    rows = jnp.concatenate(
        [jnp.sum(s, axis=0, keepdims=True) for s in sums]
        + [jnp.zeros((gram_ref.shape[1] - len(pairs), LANES), jnp.float32)],
        axis=0,
    )
    gram_ref[...] = jnp.broadcast_to(rows[None], gram_ref.shape)


def combine_kernel(count_all, gram_ref, krylov_ref, vectors_ref, alpha_ref, beta_ref):
    total = jnp.sum(jnp.sum(gram_ref[...], axis=0), axis=1, keepdims=True) * (1.0 / count_all)
    pairs = [(i, j) for i in range(STEPS + 1) for j in range(i, STEPS + 1)]
    gram = {}
    for n, (i, j) in enumerate(pairs):
        gram[i, j] = gram[j, i] = total[n : n + 1, :]

    def product(x, y):
        return sum(x[i] * (sum(gram[i, j] * y[j] for j in range(len(y)))) for i in range(len(x)))

    def raised(x):
        return [jnp.zeros_like(x[0])] + x

    def less(x, scale, y):
        return [
            x[i] - scale * y[i] if i < len(y) else x[i] for i in range(len(x))
        ]

    current = [jnp.ones_like(total[0:1, :])]
    previous = None
    square = product(current, current) + EPSILON
    scale = square
    alphas, polynomials, scales, betas = [], [], [], []
    for step in range(STEPS):
        image = raised(current)
        alpha = product(current, image) / scale
        following = less(image, alpha, current)
        if previous is not None:
            following = less(following, square, previous)
        previous, current = current, following
        square = product(current, current) / scale + EPSILON
        scale = scale * square
        alphas.append(alpha)
        betas.append(square)
        polynomials.append(current)
        scales.append(scale)
    root = jnp.sqrt(jnp.concatenate(betas, axis=0))
    inverse = [1.0 / jnp.sqrt(s) for s in scales]
    for s in range(STEPS):
        alpha_ref[s] = jnp.max(alphas[s])
        beta_ref[s] = jnp.max(root[s : s + 1, :])
    factors = [
        [jnp.broadcast_to(c * inverse[s], (SUBS, LANES)) for c in polynomials[s]]
        for s in range(STEPS)
    ]
    own_cols, length = vectors_ref.shape[2], vectors_ref.shape[3]
    for comp in range(3):
        for block in range(own_cols // SUBS):
            for c in range((length + LANES - 1) // LANES):
                start = block * SUBS * 3 * SUBS + comp * SUBS + c
                vectors = [
                    krylov_ref[s, pl.ds(start, SUBS, stride=3 * SUBS), :] for s in range(STEPS + 1)
                ]
                width = min(LANES, length - c * LANES)
                for s in range(STEPS):
                    result = sum(factors[s][i] * vectors[i] for i in range(s + 2))
                    vectors_ref[
                        s, comp, block * SUBS : (block + 1) * SUBS, c * LANES : c * LANES + width
                    ] = result[:, :width]


def per_device(state_field, direction, skin_thickness, stringer_column):
    count = lax.axis_size("circ")
    own_cols, axial_count = state_field.shape[1:]
    radius = own_cols * count / (2.0 * math.pi)
    count_all = 3.0 * own_cols * axial_count * count
    pad = own_cols
    padded = -(-axial_count // LANES) * LANES
    columns = 3 * own_cols

    local = (stringer_column - lax.axis_index("circ") * own_cols).astype(jnp.float32)
    packed = jnp.concatenate(
        [
            state_field,
            direction,
            skin_thickness[None],
            jnp.broadcast_to(local[:, None, None], (1, own_cols, axial_count)),
        ],
        axis=0,
    )
    packed = jnp.pad(packed, ((0, 0), (0, 0), (0, padded - axial_count))).transpose(1, 0, 2)
    left = lax.ppermute(
        packed[own_cols - HALO :], "circ", [(i, (i + 1) % count) for i in range(count)]
    )
    right = lax.ppermute(
        packed[:HALO], "circ", [((i + 1) % count, i) for i in range(count)]
    )
    krylov, gram = pl.pallas_call(
        functools.partial(krylov_kernel, own_cols, pad, radius),
        out_shape=(
            jax.ShapeDtypeStruct((STEPS + 1, own_cols * 3 * SUBS, LANES), jnp.float32),
            jax.ShapeDtypeStruct((count, 16, LANES), jnp.float32),
        ),
        in_specs=[pl.BlockSpec(memory_space=pltpu.VMEM)] * 3,
        out_specs=(pl.BlockSpec(memory_space=pltpu.VMEM),) * 2,
        scratch_shapes=[
            pltpu.VMEM((columns * SUBS * SUBS, LANES), jnp.float32),
            pltpu.VMEM((11, columns, 2, SUBS, LANES), jnp.float32),
            pltpu.VMEM((10, columns, 2, SUBS, LANES), jnp.float32),
            pltpu.VMEM((columns, 2, 4, 8, SUBS, LANES), jnp.float32),
            pltpu.VMEM((STEPS, columns, 3, SUBS, LANES), jnp.float32),
            pltpu.VMEM((2, 9, SUBS, LANES), jnp.float32),
            pltpu.VMEM((3, 2, 2, SUBS, LANES), jnp.float32),
        ],
        compiler_params=pltpu.CompilerParams(vmem_limit_bytes=48 * 1024 * 1024),
        name="krylov",
    )(left, packed, right)
    gram = lax.all_to_all(gram, "circ", 0, 0, tiled=True)
    return pl.pallas_call(
        functools.partial(combine_kernel, count_all),
        out_shape=(
            jax.ShapeDtypeStruct((STEPS, 3, own_cols, axial_count), jnp.float32),
            jax.ShapeDtypeStruct((STEPS,), jnp.float32),
            jax.ShapeDtypeStruct((STEPS,), jnp.float32),
        ),
        in_specs=[pl.BlockSpec(memory_space=pltpu.VMEM)] * 2,
        out_specs=(
            pl.BlockSpec(memory_space=pltpu.VMEM),
            pl.BlockSpec(memory_space=pltpu.SMEM),
            pl.BlockSpec(memory_space=pltpu.SMEM),
        ),
        name="combine",
    )(gram, krylov)


def solution(mesh):
    in_specs = (P("group", "circ", None), P("group", "circ", None), P("circ", None), P("circ"))
    out_specs = (P("group", None, "circ", None), P("group"), P("group"))
    return jax.shard_map(
        per_device, mesh=mesh, in_specs=in_specs, out_specs=out_specs, check_vma=False
    )
```

time: 332 us -> 65.3 us (0.20); the launches traced: 326 us -> 65 us
  blocking collectives: 128 us -> 11.2 us
  local copies, waits for them, and re-layouts: 92.6 us -> 2.9 us
  other arithmetic: 78.5 us -> 0.12 us
  Pallas kernels: 0 us -> 36.3 us
  loops' own time: 9.1 us -> 0 us
  starting transfers between devices: 9.86 us -> 5.53 us
    psum x4 -> x0, blocking collectives: 128 us -> none  [the longest x3 98.3 us: joined_step(): lax.psum((jnp.sum(raw_vector * raw_vector), jnp.sum(raw_vector * image_ra...]
    while x399 -> x0, local copies, waits for them, and re-layouts: 85.4 us -> none
    mul x574 -> x0, other arithmetic: 47.7 us -> none  [the longest x354 23.2 us: circ_put(): summed = summed + jnp.pad(weight * combined, pad_widths)]
    pallas_call x0 -> x2, Pallas kernels: none -> 36.3 us  [the longest x1 34 us: per_device(): pl.pallas_call(functools.partial(krylov_kernel, own_cols, pad, radius), o...]
    div x19 -> x0, other arithmetic: 11.6 us -> none  [the longest x16 11.1 us: state_point(): bending = inverse * thickness ** 3 / 12.0]
    all_to_all x0 -> x1, blocking collectives: none -> 11.2 us  [per_device(): gram = lax.all_to_all(gram, 'circ', 0, 0, tiled=True)]
    another operation x1 -> x0, loops' own time: 9.1 us -> none  [per_device(): final_carry, stacked = lax.scan(joined_step, start, None, length=STEPS)]
    reduce_sum x8 -> x0, other arithmetic: 7.98 us -> none  [the longest x4 5.05 us: joined_step(): jnp.sum(raw_vector * raw_vector)]
  transfers between devices with their start and end apart: 8 -> 2, of which waited for: 3 -> 2; matrix products, arithmetic and copies ran while one was open for 2% -> 0% of each run, Pallas kernels for 0% -> 0%
where the time goes in v1:
time: 65.3 us; the launch traced here: 65 us
  Pallas kernels  36.3 us (56%)
  blocking collectives  11.2 us (17%)
  waiting for transfers between devices  7.66 us (12%)
  starting transfers between devices  5.53 us (8%)
  local copies, waits for them, and re-layouts  2.9 us (4%)
  between operations  1.35 us (2%)
    pallas_call x1, Pallas kernels, per_device(): pl.pallas_call(functools.partial(krylov_kernel, own_cols, pad, radius), o...  34 us
    all_to_all x1, blocking collectives, per_device(): gram = lax.all_to_all(gram, 'circ', 0, 0, tiled=True)  11.2 us
    ppermute x1, starting transfers between devices, per_device(): lax.ppermute(packed[:HALO], 'circ', [((i + 1) % count, i) for i in range(...  5.53 us
    ppermute x1, waiting for transfers between devices, per_device(): lax.ppermute(packed[own_cols - HALO:], 'circ', [(i, (i + 1) % count) for...  4.6 us
    ppermute x1, waiting for transfers between devices, per_device(): lax.ppermute(packed[:HALO], 'circ', [((i + 1) % count, i) for i in range(...  3.05 us
    pallas_call x1, Pallas kernels, per_device(): pl.pallas_call(functools.partial(combine_kernel, count_all), out_shape=(j...  2.28 us
    unnamed x6, local copies, waits for them, and re-layouts  1.96 us
  transfers between devices with their start and end apart: 2, of which 2 were waited for; matrix products, arithmetic and copies ran while one was open for 0% of the time, Pallas kernels for 0%

profile of v1, /device:TPU:0, one launch (start us, length us, event | category | flops | bytes accessed | tf_op | source)
XLA Modules:
  0.0 65.0 jit_solution(1529061396016987217)
XLA Ops:
  1.3 0.8 %broadcast_in_dim.11 = f32[1,16,515]{2,0,1:T(1,128)S(1)} reshape(f32[16,515]{1,0:T(8,128)} %param.6) | data formatting | bytes 65920 | tf_op jit(solution)/shard_map/broadcast_in_dim | solution.py:555
  2.1 0.0 copy-start.1
  2.1 1.0 %copy.7 = f32[3,16,515]{2,0,1:T(4,128)S(1)} copy(f32[3,16,515]{2,1,0:T(8,128)} %param.4) | data formatting | bytes 197760 | tf_op args[0]
  3.1 0.0 copy-done.1
  3.1 0.1 copy.8
  3.2 0.1 pad.8.clone
  3.3 0.1 maximum_maximum_fusion
  3.5 5.5 %collective-permute-start.1 = (f32[9,8,640]{2,1,0:T(8,128)S(1)}, f32[9,8,640]{2,1,0:T(8,128)S(1)}, u32[]{:S(2)}, u32[]{:S(2)}) collective-permute-start(f32[9,8,640]{2,1,0:T(8,128)S(1)} %get-tuple-element.7), channel_id=1, source_target_pairs={{1,0},{2,1},{3,2},{4,3},{5,4},{6,5},{7,6},{8,7},{9,8},{10,9},{11,1... | collective-permute-start | bytes 552968 | tf_op jit(solution)/shard_map/ppermute | solution.py:564
  9.0 0.0 collective-permute-start
  9.0 3.1 %collective-permute-done.1.right_ref = f32[9,8,640]{2,1,0:T(8,128)S(1)} collective-permute-done((f32[9,8,640]{2,1,0:T(8,128)S(1)}, f32[9,8,640]{2,1,0:T(8,128)S(1)}, u32[]{:S(2)}, u32[]{:S(2)}) %collective-permute-start.1) | collective-permute-done | bytes 184352 | tf_op jit(solution)/shard_map/ppermute | solution.py:564
  12.0 4.6 %collective-permute-done.left_ref = f32[9,8,640]{2,1,0:T(8,128)S(1)} collective-permute-done((f32[9,8,640]{2,1,0:T(8,128)S(1)}, f32[9,8,640]{2,1,0:T(8,128)S(1)}, u32[]{:S(2)}, u32[]{:S(2)}) %collective-permute-start) | collective-permute-done | bytes 184352 | tf_op jit(solution)/shard_map/ppermute | solution.py:561
  16.6 34.0 %krylov.1 = (f32[4,384,128]{2,1,0:T(8,128)S(1)}, f32[16,16,128]{2,1,0:T(8,128)S(1)}) custom-call(f32[9,8,640]{2,1,0:T(8,128)S(1)} %collective-permute-done.left_ref, f32[16,8,640]{2,1,0:T(8,128)S(1)} %pad_bitcast_fusion.own_ref, f32[9,8,640]{2,1,0:T(8,128)S(1)} %collective-permute-done.1.right_ref), custom_call_target="tpu_custom_call" | custom-call | tf_op jit(solution)/shard_map/krylov/pallas_call | solution.py:567
  50.7 0.0 copy-start
  50.7 0.9 %copy-done = f32[4,384,128]{2,1,0:T(8,128)} copy-done((f32[4,384,128]{2,1,0:T(8,128)}, f32[4,384,128]{2,1,0:T(8,128)S(1)}, u32[]{:S(2)}) %copy-start) | copy-done | bytes 786456
  51.6 11.2 %all_to_all.5.gram_ref = f32[16,16,128]{2,1,0:T(8,128)} all-to-all(f32[16,16,128]{2,1,0:T(8,128)S(1)} %get-tuple-element.5), channel_id=1, replica_groups=mesh['group'=2,'circ'=16] {'circ'}, dimensions={0} | all-to-all | bytes 262144 | tf_op jit(solution)/shard_map/all_to_all | solution.py:587
  62.8 2.3 %combine.1 = (f32[3,3,16,515]{3,2,1,0:T(8,128)}, f32[3]{0:T(128)}, f32[3]{0:T(128)}) custom-call(f32[16,16,128]{2,1,0:T(8,128)} %all_to_all.5.gram_ref, f32[4,384,128]{2,1,0:T(8,128)} %copy-done), custom_call_target="tpu_custom_call" | custom-call | tf_op jit(solution)/shard_map/combine/pallas_call | solution.py:588
  (2 shorter events, 0.1 us)
Async XLA Ops:
  2.1 1.0 %copy-start.1 = (f32[3,16,515]{2,1,0:T(8,128)S(1)}, f32[3,16,515]{2,1,0:T(8,128)}, u32[]{:S(2)}) copy-start(f32[3,16,515]{2,1,0:T(8,128)} %param.5) | copy-start | bytes 296644
  3.5 8.6 %collective-permute-start.1 = (f32[9,8,640]{2,1,0:T(8,128)S(1)}, f32[9,8,640]{2,1,0:T(8,128)S(1)}, u32[]{:S(2)}, u32[]{:S(2)}) collective-permute-start(f32[9,8,640]{2,1,0:T(8,128)S(1)} %get-tuple-element.7), channel_id=1, source_target_pairs={{1,0},{2,1},{3,2},{4,3},{5,4},{6,5},{7,6},{8,7},{9,8},{10,9},{11,1... | collective-permute-start | bytes 552968 | tf_op jit(solution)/shard_map/ppermute | solution.py:564
  9.0 7.7 %collective-permute-start = (f32[9,8,640]{2,1,0:T(8,128)S(1)}, f32[9,8,640]{2,1,0:T(8,128)S(1)}, u32[]{:S(2)}, u32[]{:S(2)}) collective-permute-start(f32[9,8,640]{2,1,0:T(8,128)S(1)} %get-tuple-element.8), channel_id=1, source_target_pairs={{0,1},{1,2},{2,3},{3,4},{4,5},{5,6},{6,7},{7,8},{8,9},{9,10},{10,1... | collective-permute-start | bytes 552968 | tf_op jit(solution)/shard_map/ppermute | solution.py:561
  50.7 0.9 %copy-start = (f32[4,384,128]{2,1,0:T(8,128)}, f32[4,384,128]{2,1,0:T(8,128)S(1)}, u32[]{:S(2)}) copy-start(f32[4,384,128]{2,1,0:T(8,128)S(1)} %get-tuple-element.6.krylov_ref) | copy-start | bytes 2359300

commit v2 on v1

v2 whole, which is shorter than its diff:
```python
import functools
import math

import jax
import jax.numpy as jnp
from jax import lax
from jax.experimental import pallas as pl
from jax.experimental.pallas import tpu as pltpu
from jax.sharding import PartitionSpec as P

STEPS = 3

POISSON = 0.3
EPSILON = 1e-06
STRINGER_AXIAL = 40.0
STRINGER_BENDING = 20.0
END_STIFF = 4.0

LANES = 128
SUBS = 8
HALF = 4
HALO = 3 * STEPS

A1, B1, C0, C1, C2, DA0, DB0, DC0, DC1, DDC0, H0 = range(11)
F01, F00, F10, F11, F20, F20Q, F20L, F21, F21Q, F22 = range(10)
S_WX, S_WS, S_NX, S_NS, S_NG, S_A, S_AG, S_D = range(8)


def gauss_rule():
    inner_root = math.sqrt(3.0 / 7.0 - 2.0 / 7.0 * math.sqrt(6.0 / 5.0))
    outer_root = math.sqrt(3.0 / 7.0 + 2.0 / 7.0 * math.sqrt(6.0 / 5.0))
    weight_inner = (18.0 + math.sqrt(30.0)) / 72.0
    weight_outer = (18.0 - math.sqrt(30.0)) / 72.0
    points = [
        0.5 - 0.5 * outer_root,
        0.5 - 0.5 * inner_root,
        0.5 + 0.5 * inner_root,
        0.5 + 0.5 * outer_root,
    ]
    return points, [weight_outer, weight_inner, weight_inner, weight_outer]


def cubic(t):
    s = 1.0 - t
    return [
        s**3 / 6.0,
        (3.0 * t**3 - 6.0 * t**2 + 4.0) / 6.0,
        (-3.0 * t**3 + 3.0 * t**2 + 3.0 * t + 1.0) / 6.0,
        t**3 / 6.0,
    ]


def quadratic(t):
    return [(1.0 - t) ** 2 / 2.0, -(t**2) + t + 0.5, t**2 / 2.0]


POINTS, WEIGHTS = gauss_rule()


def take4(z):
    p03, m03, p12, m12 = z[0] + z[3], z[0] - z[3], z[1] + z[2], z[1] - z[2]

    def at(t, scale=1.0):
        b = [scale * x for x in cubic(t)]
        even = p03 * (0.5 * (b[0] + b[3])) + p12 * (0.5 * (b[1] + b[2]))
        odd = m03 * (0.5 * (b[0] - b[3])) + m12 * (0.5 * (b[1] - b[2]))
        return even, odd

    return at


def take3(d):
    p, m = d[0] + d[2], d[0] - d[2]

    def at(t, scale=1.0):
        q = [scale * x for x in quadratic(t)]
        return p * (0.5 * (q[0] + q[2])) + d[1] * q[1], m * (0.5 * (q[0] - q[2]))

    return at


def take2(g):
    even, m = 0.5 * (g[0] + g[1]), g[0] - g[1]

    def at(t):
        return even, m * (0.5 - t)

    return at


def both(pair):
    return pair[0] + pair[1], pair[0] - pair[1]


def merged(first, second):
    return first[0] + second[0], first[1] + second[1]


def put4(pairs, scale=1.0):
    sums = None
    for t, (one, two) in pairs:
        s, d = one + two, one - two
        b = [scale * x for x in cubic(t)]
        terms = [
            s * (0.5 * (b[0] + b[3])),
            d * (0.5 * (b[0] - b[3])),
            s * (0.5 * (b[1] + b[2])),
            d * (0.5 * (b[1] - b[2])),
        ]
        sums = terms if sums is None else [x + y for x, y in zip(sums, terms)]
    e03, o03, e12, o12 = sums
    return [e03 + o03, e12 + o12, e12 - o12, e03 - o03]


def put3(pairs):
    sums = None
    for t, (one, two) in pairs:
        s, d = one + two, one - two
        q = quadratic(t)
        terms = [s * (0.5 * (q[0] + q[2])), d * (0.5 * (q[0] - q[2])), s * q[1]]
        sums = terms if sums is None else [x + y for x, y in zip(sums, terms)]
    even, odd, middle = sums
    return [even + odd, middle, even - odd]


def put2(pairs):
    even, odd = None, None
    for t, (one, two) in pairs:
        s, d = one + two, (one - two) * (0.5 - t)
        even = s if even is None else even + s
        odd = d if odd is None else odd + d
    even = 0.5 * even
    return [even + odd, even - odd]


VECTOR = 11
TAPS = ((F01, 4), (F00, 3), (F10, 3), (F11, 4), (F20, 4), (F20Q, 3), (F20L, 2), (F21, 4), (F21Q, 3), (F22, 4))
PAIRS = [(i, j) for i in range(STEPS + 1) for j in range(i, STEPS + 1)]


def loop(low, high, body, carry, unroll=1):
    rounds = (high - low) // unroll

    def several(i, carry):
        start = low + i * unroll
        return body([start + u for u in range(unroll)], carry)

    if rounds > 0:
        carry = lax.fori_loop(0, rounds, several, carry)
    rest = list(range(low + rounds * unroll, high))
    return body(rest, carry) if rest else carry


def pack_kernel(own_cols, state_ref, direction_ref, thick_ref, column_ref, own_ref, head_ref, tail_ref):
    length = thick_ref.shape[1]
    chunks = own_ref.shape[0] // (own_cols * SUBS)
    local = lax.rem(column_ref[0], own_cols).astype(jnp.float32)

    def put(f, rows, part, c):
        own_ref[pl.ds((c * own_cols + rows) * SUBS + f, SUBS, stride=SUBS), :] = part
        for ref, low in ((head_ref, 0), (tail_ref, own_cols - HALO)):
            start, stop = max(rows, low), min(rows + SUBS, low + HALO)
            if stop - start == SUBS:
                row = (c * HALO + start - low) * SUBS + f
                ref[pl.ds(row, SUBS, stride=SUBS), :] = part
            else:
                for col in range(start, stop):
                    row = (c * HALO + col - low) * SUBS + f
                    ref[row : row + 1, :] = part[col - rows : col - rows + 1]

    sources = [(state_ref.at[i], i) for i in range(3)]
    sources += [(direction_ref.at[i], 3 + i) for i in range(3)] + [(thick_ref, 6)]
    for rows in range(0, own_cols, SUBS):
        for source, f in sources:
            for c in range(chunks):
                width = min(LANES, length - c * LANES)
                part = source[rows : rows + SUBS, c * LANES : c * LANES + width]
                if width < LANES:
                    fill = jnp.zeros((SUBS, LANES - width), jnp.float32)
                    part = jnp.concatenate([part, fill], axis=1)
                put(f, rows, part, c)
        put(7, rows, jnp.full((SUBS, LANES), local), 0)


class Shell:
    def __init__(self, own_cols, pad, radius, field_ref, take_ref, acc_ref, state_ref, table_ref):
        self.own_cols, self.pad, self.radius = own_cols, pad, radius
        self.field_ref, self.take_ref, self.acc_ref = field_ref, take_ref, acc_ref
        self.state_ref, self.table_ref = state_ref, table_ref
        self.sub = lax.broadcasted_iota(jnp.int32, (SUBS, LANES), 0)
        self.lane = lax.broadcasted_iota(jnp.int32, (SUBS, LANES), 1)
        self.low = self.sub < HALF
        self.zero = jnp.zeros((SUBS, LANES), jnp.float32)
        self.nothing = tuple((self.zero,) * 5 for _ in range(2))
        for h in range(2):
            first, second = POINTS[h], POINTS[3 - h]
            rows = (
                list(zip(cubic(first), cubic(second)))
                + list(zip(quadratic(first), quadratic(second)))
                + [(1.0 - first, 1.0 - second), (first, second)]
            )
            for i, (x, y) in enumerate(rows):
                table_ref[h, i] = jnp.where(self.low, jnp.float32(x), jnp.float32(y))

    def spread(self, source, offset, count):
        for c in range(source.shape[0] // (count * SUBS)):
            for i in range(count):
                start = (offset + i) * SUBS * SUBS + c
                row = (c * count + i) * SUBS
                self.field_ref[pl.ds(start, SUBS, stride=SUBS), :] = source[row : row + SUBS, :]

    def field(self, col, index):
        start = col * (SUBS * SUBS) + index * SUBS
        if not isinstance(start, int):
            start = pl.multiple_of(start, SUBS)
        return self.field_ref[pl.ds(start, SUBS), :]

    def shifted(self, v):
        following = pltpu.roll(v, SUBS - 1, 0)
        shifts = [v] + [
            pltpu.roll(jnp.where(self.lane < o, following, v), LANES - o, 1) for o in range(1, 4)
        ]
        return [jnp.where(self.low, z, pltpu.roll(z, HALF, 0)) for z in shifts]

    def value(self, z, h):
        return sum(self.table_ref[h, o] * z[o] for o in range(4))

    def slope(self, d, h):
        return sum(self.table_ref[h, 4 + o] * d[o] for o in range(3))

    def curve(self, g, h):
        return self.table_ref[h, 7] * g[0] + self.table_ref[h, 8] * g[1]

    def axial_take(self, low, high, load, base, carry, thick=False, unroll=2):
        take_ref = self.take_ref

        def differences(z):
            return [z[o + 1] - z[o] for o in range(len(z) - 1)]

        def body(cols, carry):
            loaded = [[load(col, i) for i in range(4 if thick else 3)] for col in cols]
            for col, vectors in zip(cols, loaded):
                za, zb, zc = (self.shifted(v) for v in vectors[:3])
                da, db, dc = differences(za), differences(zb), differences(zc)
                gc = differences(dc)
                zh = self.shifted(vectors[3]) if thick else None
                out = []
                for h in range(2):
                    old_a0, old_b0, old_c0, old_c1, old_dc0 = carry[h]
                    a0, b0, c0 = self.value(za, h), self.value(zb, h), self.value(zc, h)
                    c1, dc0 = self.slope(dc, h), c0 - old_c0
                    take_ref[base + A1, col, h] = self.slope(da, h)
                    take_ref[base + B1, col, h] = self.slope(db, h)
                    take_ref[base + C0, col, h] = c0
                    take_ref[base + C1, col, h] = c1
                    take_ref[base + DA0, col - 1, h] = a0 - old_a0
                    take_ref[base + DB0, col - 1, h] = b0 - old_b0
                    take_ref[base + DC0, col - 1, h] = dc0
                    if thick:
                        take_ref[base + H0, col, h] = self.value(zh, h)
                    else:
                        take_ref[base + C2, col, h] = self.curve(gc, h)
                        take_ref[base + DC1, col - 1, h] = c1 - old_c1
                        take_ref[base + DDC0, col - 2, h] = dc0 - old_dc0
                    out.append((a0, b0, c0, c1, dc0))
                carry = tuple(out)
            return carry

        return loop(low, high, body, carry, unroll)

    def takes(self, name, k, h, taps):
        return [self.take_ref[name, k + o, h] for o in range(taps)]

    def prepare(self, low, high):
        inverse = 1.0 / (1.0 - POISSON * POISSON)
        takes, state_ref = self.takes, self.state_ref

        def body(cols, unused):
            (k,) = cols
            for h in range(2):
                u1 = take4(takes(A1, k, h, 4))
                us = take3(takes(DA0, k, h, 3))
                vs = take3(takes(DB0, k, h, 3))
                vx = take4(takes(B1, k, h, 4))
                w0 = take4(takes(C0, k, h, 4))
                w1 = take4(takes(C1, k, h, 4))
                ws = take3(takes(DC0, k, h, 3))
                h0 = take4(takes(H0, k, h, 4))
                for p in range(2):
                    t = POINTS[p]
                    weight = WEIGHTS[p] * WEIGHTS[h]
                    along = both(u1(t))
                    across = both(merged(vs(t), w0(t, 1.0 / self.radius)))
                    shear = both(merged(us(t), vx(t)))
                    tilt_x, tilt_s, thick = both(w1(t)), both(ws(t)), both(h0(t))
                    for q in range(2):
                        wx, wc, th = tilt_x[q], tilt_s[q], thick[q]
                        ex = along[q] + 0.5 * wx * wx
                        es = across[q] + 0.5 * wc * wc
                        g = shear[q] + wx * wc
                        a = th * (inverse * weight)
                        ag = a * (0.5 * (1.0 - POISSON))
                        point = p if q == 0 else 3 - p
                        state_ref[k, h, point, S_WX] = wx
                        state_ref[k, h, point, S_WS] = wc
                        state_ref[k, h, point, S_NX] = a * (ex + POISSON * es)
                        state_ref[k, h, point, S_NS] = a * (POISSON * ex + es)
                        state_ref[k, h, point, S_NG] = ag * g
                        state_ref[k, h, point, S_A] = a
                        state_ref[k, h, point, S_AG] = ag
                        state_ref[k, h, point, S_D] = a * (th * th) * (1.0 / 12.0)
            return unused

        loop(low, high, body, 0)

    def clear(self, low, count=None):
        for name, taps in TAPS:
            for o in range(taps - 1 if count is None else count):
                for h in range(2):
                    self.acc_ref[name, low + o, h] = self.zero

    def spans(self, low, high, fresh=True):
        takes, state_ref, acc_ref = self.takes, self.state_ref, self.acc_ref

        def add(name, k, h, parts):
            for o, part in enumerate(parts):
                if fresh and o == len(parts) - 1:
                    acc_ref[name, k + o, h] = part
                else:
                    acc_ref[name, k + o, h] += part

        def body(cols, unused):
            (k,) = cols
            for h in range(2):
                a1 = take4(takes(VECTOR + A1, k, h, 4))
                b1 = take4(takes(VECTOR + B1, k, h, 4))
                c0 = take4(takes(VECTOR + C0, k, h, 4))
                c1 = take4(takes(VECTOR + C1, k, h, 4))
                c2 = take4(takes(VECTOR + C2, k, h, 4))
                as0 = take3(takes(VECTOR + DA0, k, h, 3))
                bs0 = take3(takes(VECTOR + DB0, k, h, 3))
                cs0 = take3(takes(VECTOR + DC0, k, h, 3))
                cx0 = take3(takes(VECTOR + DC1, k, h, 3))
                cc0 = take2(takes(VECTOR + DDC0, k, h, 2))
                parts = []
                for p in range(2):
                    t = POINTS[p]
                    along = both(a1(t))
                    across = both(merged(bs0(t), c0(t, 1.0 / self.radius)))
                    shear = both(merged(as0(t), b1(t)))
                    tilt_x, tilt_s = both(c1(t)), both(cs0(t))
                    bend_x, bend_s = both(c2(t)), both(cc0(t))
                    twist = both(cx0(t, 2.0 * (1.0 - POISSON)))
                    results = []
                    for q in range(2):
                        point = p if q == 0 else 3 - p
                        wx, wc = state_ref[k, h, point, S_WX], state_ref[k, h, point, S_WS]
                        cx, cs = tilt_x[q], tilt_s[q]
                        ex = along[q] + wx * cx
                        es = across[q] + wc * cs
                        g = shear[q] + wx * cs + wc * cx
                        a = state_ref[k, h, point, S_A]
                        fx = a * (ex + POISSON * es)
                        fs = a * (POISSON * ex + es)
                        fg = state_ref[k, h, point, S_AG] * g
                        d = state_ref[k, h, point, S_D]
                        mx = d * (bend_x[q] + POISSON * bend_s[q])
                        ms = d * (POISSON * bend_x[q] + bend_s[q])
                        mg = d * twist[q]
                        ng = state_ref[k, h, point, S_NG]
                        sx = fx * wx + fg * wc + state_ref[k, h, point, S_NX] * cx + ng * cs
                        ss = fs * wc + fg * wx + state_ref[k, h, point, S_NS] * cs + ng * cx
                        results.append((fx, fs, fg, mx, ms, mg, sx, ss))
                    parts.append((t, list(zip(*results))))

                def pick(i):
                    return [(t, values[i]) for t, values in parts]

                add(F01, k, h, put4(pick(0)))
                add(F00, k, h, put3(pick(2)))
                add(F10, k, h, put3(pick(1)))
                add(F11, k, h, put4(pick(2)))
                add(F20, k, h, put4(pick(1), 1.0 / self.radius))
                add(F20Q, k, h, put3(pick(7)))
                add(F20L, k, h, put2(pick(4)))
                add(F21, k, h, put4(pick(6)))
                add(F21Q, k, h, put3(pick(5)))
                add(F22, k, h, put4(pick(3)))
            return unused

        loop(low, high, body, 0)

    def axial_put(self, zeroth, first, second):
        table_ref, lane, low = self.table_ref, self.lane, self.low
        t = [sum(table_ref[h, o] * zeroth[h] for h in range(2)) for o in range(4)]
        r = [sum(table_ref[h, 4 + o] * first[h] for h in range(2)) for o in range(3)]
        t = [t[0] - r[0], t[1] + (r[0] - r[1]), t[2] + (r[1] - r[2]), t[3] + r[2]]
        if second is not None:
            l0, l1 = (sum(table_ref[h, 7 + o] * second[h] for h in range(2)) for o in range(2))
            t = [t[0] + l0, t[1] + (l1 - 2.0 * l0), t[2] + (l0 - 2.0 * l1), t[3] + l1]
        stay, cross = t[0], self.zero
        for o in range(1, 4):
            moved = pltpu.roll(t[o], o, 1)
            stay = stay + jnp.where(lane < o, 0.0, moved)
            cross = cross + jnp.where(lane < o, moved, 0.0)
        stay = jnp.where(low, stay + pltpu.roll(stay, HALF, 0), 0.0)
        cross = jnp.where(low, cross + pltpu.roll(cross, HALF, 0), 0.0)
        return stay + pltpu.roll(cross, 1, 0)

    def end_part(self, v):
        corners = ((self.sub == 0) | (self.sub == HALF)) & (self.lane == 0)
        row = (v + 4.0 * pltpu.roll(v, LANES - 1, 1) + pltpu.roll(v, LANES - 2, 1)) * (
            END_STIFF / 36.0
        )
        row = jnp.where(corners, row, 0.0)
        return row + 4.0 * pltpu.roll(row, 1, 1) + pltpu.roll(row, 2, 1)

    def gather(self, low, high, load, image_ref, step, unroll=2):
        acc_ref, halves = self.acc_ref, range(2)

        def back(name, col, h):
            return acc_ref[name, col - 1, h] - acc_ref[name, col, h]

        def body(cols, unused):
            work = []
            for col in cols:
                zeroth = [
                    [back(F00, col, h) for h in halves],
                    [back(F10, col, h) for h in halves],
                    [
                        acc_ref[F20, col, h]
                        + back(F20Q, col, h)
                        + (acc_ref[F20L, col - 2, h] - acc_ref[F20L, col - 1, h])
                        - back(F20L, col, h)
                        for h in halves
                    ],
                ]
                first = [
                    [acc_ref[F01, col, h] for h in halves],
                    [acc_ref[F11, col, h] for h in halves],
                    [acc_ref[F21, col, h] + back(F21Q, col, h) for h in halves],
                ]
                second = [None, None, [acc_ref[F22, col, h] for h in halves]]
                work.append((zeroth, first, second, [load(col, i) for i in range(3)]))
            images = [
                [
                    self.axial_put(zeroth[i], first[i], second[i]) + self.end_part(v[i])
                    for i in range(3)
                ]
                for zeroth, first, second, v in work
            ]
            for col, image in zip(cols, images):
                for i in range(3):
                    image_ref[step, col, i] = image[i]
            return unused

        loop(low, high, body, 0, unroll)


def own_kernel(own_cols, pad, radius, own_ref, field_ref, take_ref, acc_ref, state_ref, carry_ref, table_ref):
    shell = Shell(own_cols, pad, radius, field_ref, take_ref, acc_ref, state_ref, table_ref)
    for col in range(pad, pad + own_cols):
        for i in range(3, 6):
            start = col * SUBS * SUBS + i * SUBS
            field_ref[start : start + SUBS, :] = shell.zero
    shell.spread(own_ref, pad, own_cols)
    stop = pad + own_cols
    carry = shell.axial_take(pad, stop, lambda c, i: shell.field(c, (0, 1, 2, 6)[i]), 0, shell.nothing, thick=True)
    for h in range(2):
        for i in range(5):
            carry_ref[0, h, i] = carry[h][i]
    carry = shell.axial_take(pad, stop, lambda c, i: shell.field(c, 3 + i), VECTOR, shell.nothing)
    for h in range(2):
        for i in range(5):
            carry_ref[1, h, i] = carry[h][i]
    shell.prepare(pad, stop - 3)
    shell.clear(pad)
    shell.spans(pad, stop - 3)


def krylov_kernel(
    own_cols,
    pad,
    radius,
    left_ref,
    right_ref,
    own_ref,
    carry_ref,
    field_in,
    take_in,
    acc_in,
    state_in,
    krylov_ref,
    gram_ref,
    field_ref,
    take_ref,
    acc_ref,
    state_ref,
    image_ref,
    table_ref,
    line_ref,
):
    shell = Shell(own_cols, pad, radius, field_ref, take_ref, acc_ref, state_ref, table_ref)
    field, zero = shell.field, shell.zero
    stop = pad + own_cols
    shell.spread(left_ref, pad - HALO, HALO)
    shell.spread(right_ref, stop, HALO)

    for index, base, names in ((0, 0, (0, 1, 2, 6)), (1, VECTOR, (3, 4, 5))):
        def load(col, i, names=names):
            return field(col, names[i])

        thick = index == 0
        shell.axial_take(pad - HALO, pad + 2, load, base, shell.nothing, thick=thick)
        carry = tuple(tuple(carry_ref[index, h, i] for i in range(5)) for h in range(2))
        shell.axial_take(stop, stop + HALO, load, base, carry, thick=thick)
    shell.prepare(pad - HALO, pad)
    shell.prepare(stop - 3, stop + HALO - 3)

    stringers = []
    for i, source in enumerate((left_ref, own_ref, right_ref)):
        column = jnp.max(source[7:8, :]).astype(jnp.int32)
        stringers.append(column + (pad + (i - 1) * own_cols))
    marks = (1.0 / 6.0, 4.0 / 6.0, 1.0 / 6.0)

    def line(name, column, h):
        return sum(marks[j] * take_ref[name, column + j, h] for j in range(3))

    for i, column in enumerate(stringers):
        for h in range(2):
            along, tilt = line(A1, column, h), line(C1, column, h)
            line_ref[i, h, 0] = along + 0.5 * tilt * tilt
            line_ref[i, h, 1] = tilt

    for step in range(STEPS):
        reach = HALO - 3 * step
        first, last = pad - reach, stop + reach - 3

        def load(col, index, step=step):
            if step == 0:
                return field(col, 3 + index)
            return image_ref[step - 1, col, index]

        if step == 0:
            shell.clear(first, reach)
            shell.spans(first, pad, fresh=False)
            shell.spans(stop - 3, last)
        else:
            shell.axial_take(first, last + 3, load, VECTOR, shell.nothing)
            shell.clear(first)
            shell.spans(first, last)

        for i, column in enumerate(stringers):
            for h in range(2):
                weight = jnp.float32(WEIGHTS[h])
                stretch, tilt = line_ref[i, h, 0], line_ref[i, h, 1]
                slope_c = line(VECTOR + C1, column, h)
                d_stretch = line(VECTOR + A1, column, h) + tilt * slope_c
                f0 = (STRINGER_AXIAL * weight) * d_stretch
                f1 = (STRINGER_AXIAL * weight) * (d_stretch * tilt + stretch * slope_c)
                f2 = (STRINGER_BENDING * weight) * line(VECTOR + C2, column, h)
                for j in range(3):
                    acc_ref[F01, column + j, h] += marks[j] * f0
                    acc_ref[F21, column + j, h] += marks[j] * f1
                    acc_ref[F22, column + j, h] += marks[j] * f2

        shell.gather(first + 3, last, load, image_ref, step)

    def inner(cols, sums):
        sums = list(sums)
        for col in cols:
            for comp in range(3):
                vectors = [field(pad + col, 3 + comp)] + [
                    image_ref[s, pad + col, comp] for s in range(STEPS)
                ]
                for s, vector in enumerate(vectors):
                    start = pl.multiple_of(col * (3 * SUBS) + comp * SUBS, SUBS)
                    krylov_ref[s, pl.ds(start, SUBS), :] = vector
                for n, (x, y) in enumerate(PAIRS):
                    sums[n] = sums[n] + vectors[x] * vectors[y]
        return tuple(sums)

    sums = loop(0, own_cols, inner, (zero,) * len(PAIRS))
    row = jnp.zeros((1, LANES), jnp.float32)
    for n, s in enumerate(sums):
        part = jnp.sum(jnp.sum(s, axis=0, keepdims=True), axis=1, keepdims=True)
        row = jnp.where(shell.lane[0:1] == n, part, row)
    gram_ref[...] = jnp.broadcast_to(row, gram_ref.shape)


def combine_kernel(count_all, gram_ref, krylov_ref, vectors_ref, alpha_ref, beta_ref):
    row = jnp.sum(gram_ref[...], axis=0, keepdims=True) * (1.0 / count_all)
    gram = {}
    for n, (i, j) in enumerate(PAIRS):
        gram[i, j] = gram[j, i] = row[:, n : n + 1]

    def product(x, y):
        return sum(x[i] * (sum(gram[i, j] * y[j] for j in range(len(y)))) for i in range(len(x)))

    def raised(x):
        return [jnp.zeros_like(x[0])] + x

    def less(x, scale, y):
        return [
            x[i] - scale * y[i] if i < len(y) else x[i] for i in range(len(x))
        ]

    current = [jnp.ones((1, 1), jnp.float32)]
    previous = None
    square = product(current, current) + EPSILON
    scale = square
    alphas, polynomials, scales, betas = [], [], [], []
    for step in range(STEPS):
        image = raised(current)
        alpha = product(current, image) / scale
        following = less(image, alpha, current)
        if previous is not None:
            following = less(following, square, previous)
        previous, current = current, following
        square = product(current, current) / scale + EPSILON
        scale = scale * square
        alphas.append(alpha)
        betas.append(square)
        polynomials.append(current)
        scales.append(scale)
    root = jnp.sqrt(jnp.concatenate(betas, axis=0))
    inverse = [1.0 / jnp.sqrt(s) for s in scales]
    for s in range(STEPS):
        alpha_ref[s] = jnp.max(alphas[s])
        beta_ref[s] = jnp.max(root[s : s + 1, :])
    factors = [
        [jnp.broadcast_to(c * inverse[s], (SUBS, LANES)) for c in polynomials[s]]
        for s in range(STEPS)
    ]
    own_cols, length = vectors_ref.shape[2], vectors_ref.shape[3]
    for comp in range(3):
        for block in range(own_cols // SUBS):
            for c in range((length + LANES - 1) // LANES):
                start = block * SUBS * 3 * SUBS + comp * SUBS + c
                vectors = [
                    krylov_ref[s, pl.ds(start, SUBS, stride=3 * SUBS), :] for s in range(STEPS + 1)
                ]
                width = min(LANES, length - c * LANES)
                for s in range(STEPS):
                    result = sum(factors[s][i] * vectors[i] for i in range(s + 2))
                    vectors_ref[
                        s, comp, block * SUBS : (block + 1) * SUBS, c * LANES : c * LANES + width
                    ] = result[:, :width]


def per_device(state_field, direction, skin_thickness, stringer_column):
    count = lax.axis_size("circ")
    own_cols, axial_count = state_field.shape[1:]
    radius = own_cols * count / (2.0 * math.pi)
    count_all = 3.0 * own_cols * axial_count * count
    pad = own_cols
    chunks = -(-axial_count // LANES)
    columns = 3 * own_cols
    vmem = pl.BlockSpec(memory_space=pltpu.VMEM)
    smem = pl.BlockSpec(memory_space=pltpu.SMEM)

    def shape(*dims):
        return jax.ShapeDtypeStruct(dims, jnp.float32)

    def params(mebibytes):
        return pltpu.CompilerParams(vmem_limit_bytes=mebibytes * 1024 * 1024)

    packed, head, tail = pl.pallas_call(
        functools.partial(pack_kernel, own_cols),
        out_shape=(
            shape(chunks * own_cols * SUBS, LANES),
            shape(chunks * HALO * SUBS, LANES),
            shape(chunks * HALO * SUBS, LANES),
        ),
        in_specs=[vmem, vmem, vmem, smem],
        out_specs=(vmem,) * 3,
        compiler_params=params(8),
        name="pack",
    )(state_field, direction, skin_thickness, stringer_column)
    left = lax.ppermute(tail, "circ", [(i, (i + 1) % count) for i in range(count)])
    right = lax.ppermute(head, "circ", [((i + 1) % count, i) for i in range(count)])
    buffers = (
        shape(columns * SUBS * SUBS, LANES),
        shape(21, columns, 2, SUBS, LANES),
        shape(10, columns, 2, SUBS, LANES),
        shape(columns, 2, 4, 8, SUBS, LANES),
    )
    table = pltpu.VMEM((2, 9, SUBS, LANES), jnp.float32)
    *kept, carry = pl.pallas_call(
        functools.partial(own_kernel, own_cols, pad, radius),
        out_shape=buffers + (shape(2, 2, 5, SUBS, LANES),),
        in_specs=[vmem],
        out_specs=(vmem,) * 5,
        scratch_shapes=[table],
        compiler_params=params(4),
        cost_estimate=pl.CostEstimate(flops=40000000, bytes_accessed=20000000, transcendentals=0),
        name="own",
    )(packed)
    krylov, gram, *_ = pl.pallas_call(
        functools.partial(krylov_kernel, own_cols, pad, radius),
        out_shape=(shape(STEPS + 1, own_cols * 3 * SUBS, LANES), shape(count, LANES)) + buffers,
        in_specs=[vmem] * 8,
        out_specs=(vmem,) * 6,
        input_output_aliases={4: 2, 5: 3, 6: 4, 7: 5},
        scratch_shapes=[
            pltpu.VMEM((STEPS, columns, 3, SUBS, LANES), jnp.float32),
            table,
            pltpu.VMEM((3, 2, 2, SUBS, LANES), jnp.float32),
        ],
        compiler_params=params(8),
        name="krylov",
    )(left, right, packed, carry, *kept)
    gram = lax.all_to_all(gram, "circ", 0, 0, tiled=True)
    return pl.pallas_call(
        functools.partial(combine_kernel, count_all),
        out_shape=(shape(STEPS, 3, own_cols, axial_count), shape(STEPS), shape(STEPS)),
        in_specs=[vmem] * 2,
        out_specs=(vmem, smem, smem),
        compiler_params=params(8),
        name="combine",
    )(gram, krylov)


def solution(mesh):
    in_specs = (P("group", "circ", None), P("group", "circ", None), P("circ", None), P("circ"))
    out_specs = (P("group", None, "circ", None), P("group"), P("group"))
    return jax.shard_map(
        per_device, mesh=mesh, in_specs=in_specs, out_specs=out_specs, check_vma=False
    )
```

time: 65.3 us -> 47.5 us (0.73)
  Pallas kernels: 36.3 us -> 27 us
  waiting for transfers between devices: 7.66 us -> 0.01 us
    pallas_call x1, Pallas kernels: 34 us -> 20.7 us  [per_device(): pl.pallas_call(functools.partial(krylov_kernel, own_cols, pad, radius), o...]
    ppermute x2, waiting for transfers between devices: 7.66 us -> 0.01 us  [the longest x1 0.01 us: per_device(): lax.ppermute(tail, 'circ', [(i, (i + 1) % count) for i in range(count)])]
    pallas_call x1 -> x3, Pallas kernels: 2.28 us -> 6.27 us  [the longest x1 4.5 us: per_device(): pl.pallas_call(functools.partial(own_kernel, own_cols, pad, radius), out_...]
    broadcast_in_dim x1 -> x0, local copies, waits for them, and re-layouts: 0.81 us -> none  [per_device(): skin_thickness[None]]
  transfers between devices with their start and end apart: 2 -> 2, of which waited for: 2 -> 0; matrix products, arithmetic and copies ran while one was open for 0% -> 0% of each run, Pallas kernels for 0% -> 10%
where the time goes in v2:
time: 47.5 us; the launch traced here: 47.2 us
  Pallas kernels  27 us (57%)
  blocking collectives  10.7 us (23%)
  starting transfers between devices  5.59 us (12%)
  local copies, waits for them, and re-layouts  2.57 us (5%)
  between operations  1.32 us (3%)
    pallas_call x1, Pallas kernels, per_device(): pl.pallas_call(functools.partial(krylov_kernel, own_cols, pad, radius), o...  20.7 us
    all_to_all x1, blocking collectives, per_device(): gram = lax.all_to_all(gram, 'circ', 0, 0, tiled=True)  10.7 us
    ppermute x1, starting transfers between devices, per_device(): lax.ppermute(head, 'circ', [((i + 1) % count, i) for i in range(count)])  5.05 us
    pallas_call x1, Pallas kernels, per_device(): pl.pallas_call(functools.partial(own_kernel, own_cols, pad, radius), out_...  4.5 us
    unnamed x6, local copies, waits for them, and re-layouts  2.57 us
    pallas_call x1, Pallas kernels, per_device(): pl.pallas_call(functools.partial(combine_kernel, count_all), out_shape=(s...  1.64 us
  transfers between devices with their start and end apart: 2, of which 0 were waited for; matrix products, arithmetic and copies ran while one was open for 0% of the time, Pallas kernels for 10%

profile of v2, /device:TPU:0, one launch (start us, length us, event | category | flops | bytes accessed | tf_op | source)
XLA Modules:
  0.0 47.2 jit_solution(14777252110516563234)
XLA Ops:
  1.3 0.0 copy-start
  1.3 0.9 %copy-done = f32[3,16,515]{2,1,0:T(8,128)S(1)} copy-done((f32[3,16,515]{2,1,0:T(8,128)S(1)}, f32[3,16,515]{2,1,0:T(8,128)}, u32[]{:S(2)}) %copy-start) | copy-done | bytes 98904
  2.2 0.0 copy-start.1
  2.2 0.9 %copy-done.1 = f32[3,16,515]{2,1,0:T(8,128)S(1)} copy-done((f32[3,16,515]{2,1,0:T(8,128)S(1)}, f32[3,16,515]{2,1,0:T(8,128)}, u32[]{:S(2)}) %copy-start.1) | copy-done | bytes 98904
  3.1 0.0 copy-start.2
  3.1 0.8 %copy-done.2 = f32[16,515]{1,0:T(8,128)S(1)} copy-done((f32[16,515]{1,0:T(8,128)S(1)}, f32[16,515]{1,0:T(8,128)}, u32[]{:S(2)}) %copy-start.2) | copy-done | bytes 32984
  3.9 0.1 pack.1
  4.0 0.5 %collective-permute-start = (f32[360,128]{1,0:T(8,128)S(1)}, f32[360,128]{1,0:T(8,128)S(1)}, u32[]{:S(2)}, u32[]{:S(2)}) collective-permute-start(f32[360,128]{1,0:T(8,128)S(1)} %get-tuple-element.13), channel_id=1, source_target_pairs={{0,1},{1,2},{2,3},{3,4},{4,5},{5,6},{6,7},{7,8},{8,9},{9,10},{10,1... | collective-permute-start | bytes 552968 | tf_op jit(solution)/shard_map/ppermute | solution.py:680
  4.6 5.0 %collective-permute-start.1 = (f32[360,128]{1,0:T(8,128)S(1)}, f32[360,128]{1,0:T(8,128)S(1)}, u32[]{:S(2)}, u32[]{:S(2)}) collective-permute-start(f32[360,128]{1,0:T(8,128)S(1)} %get-tuple-element.14), channel_id=1, source_target_pairs={{1,0},{2,1},{3,2},{4,3},{5,4},{6,5},{7,6},{8,7},{9,8},{10,9},{11,1... | collective-permute-start | bytes 552968 | tf_op jit(solution)/shard_map/ppermute | solution.py:681
  9.6 4.5 %own.1 = (f32[3072,128]{1,0:T(8,128)S(1)}, f32[21,48,2,8,128]{4,3,2,1,0:T(8,128)S(1)}, f32[10,48,2,8,128]{4,3,2,1,0:T(8,128)S(1)}, f32[48,2,4,8,8,128]{5,4,3,2,1,0:T(8,128)S(1)}, f32[2,2,5,8,128]{4,3,2,1,0:T(8,128)S(1)}) custom-call(f32[640,128]{1,0:T(8,128)S(1)} %get-tuple-element.15.own_ref), custom_call_target="tpu_custom_call" | custom-call | flops 40000000 | bytes 20000000 | tf_op jit(solution)/shard_map/own/pallas_call | solution.py:689
  14.1 0.0 collective-permute-done.left_ref
  14.1 0.0 collective-permute-done.1.right_ref
  14.1 20.7 %krylov.1 = (f32[4,384,128]{2,1,0:T(8,128)S(1)}, f32[16,128]{1,0:T(8,128)S(1)}, f32[3072,128]{1,0:T(8,128)S(1)}, f32[21,48,2,8,128]{4,3,2,1,0:T(8,128)S(1)}, f32...) custom-call(f32[360,128]{1,0:T(8,128)S(1)} %collective-permute-done., ...), custom_call_target="tpu_custom_call", output_to_operand_aliasing={{2}: (4, {}), {3}: (5, {}), {4}: (6, {}), {5}: (7, {})} | custom-call | tf_op jit(solution)/shard_map/krylov/pallas_call | solution.py:699
  34.8 10.7 %all_to_all.11 = f32[16,1,128]{2,1,0:T(1,128)S(1)} all-to-all(f32[16,1,128]{2,1,0:T(1,128)S(1)} %bitcast.5), channel_id=1, replica_groups=mesh['group'=2,'circ'=16] {'circ'}, dimensions={0} | all-to-all | bytes 16384 | tf_op jit(solution)/shard_map/all_to_all | solution.py:713
  45.6 1.6 %combine.1 = (f32[3,3,16,515]{3,2,1,0:T(8,128)}, f32[3]{0:T(128)}, f32[3]{0:T(128)}) custom-call(f32[16,128]{1,0:T(8,128)S(1)} %bitcast.4, f32[4,384,128]{2,1,0:T(8,128)S(1)} %get-tuple-element.22.krylov_ref), custom_call_target="tpu_custom_call" | custom-call | tf_op jit(solution)/shard_map/combine/pallas_call | solution.py:714
Async XLA Ops:
  1.3 0.9 %copy-start = (f32[3,16,515]{2,1,0:T(8,128)S(1)}, f32[3,16,515]{2,1,0:T(8,128)}, u32[]{:S(2)}) copy-start(f32[3,16,515]{2,1,0:T(8,128)} %state_ref.1) | copy-start | bytes 296644
  2.2 0.9 %copy-start.1 = (f32[3,16,515]{2,1,0:T(8,128)S(1)}, f32[3,16,515]{2,1,0:T(8,128)}, u32[]{:S(2)}) copy-start(f32[3,16,515]{2,1,0:T(8,128)} %direction_ref.1) | copy-start | bytes 296644
  3.1 0.8 %copy-start.2 = (f32[16,515]{1,0:T(8,128)S(1)}, f32[16,515]{1,0:T(8,128)}, u32[]{:S(2)}) copy-start(f32[16,515]{1,0:T(8,128)} %thick_ref.1) | copy-start | bytes 98884
  4.0 10.1 %collective-permute-start = (f32[360,128]{1,0:T(8,128)S(1)}, f32[360,128]{1,0:T(8,128)S(1)}, u32[]{:S(2)}, u32[]{:S(2)}) collective-permute-start(f32[360,128]{1,0:T(8,128)S(1)} %get-tuple-element.13), channel_id=1, source_target_pairs={{0,1},{1,2},{2,3},{3,4},{4,5},{5,6},{6,7},{7,8},{8,9},{9,10},{10,1... | collective-permute-start | bytes 552968 | tf_op jit(solution)/shard_map/ppermute | solution.py:680
  4.6 9.6 %collective-permute-start.1 = (f32[360,128]{1,0:T(8,128)S(1)}, f32[360,128]{1,0:T(8,128)S(1)}, u32[]{:S(2)}, u32[]{:S(2)}) collective-permute-start(f32[360,128]{1,0:T(8,128)S(1)} %get-tuple-element.14), channel_id=1, source_target_pairs={{1,0},{2,1},{3,2},{4,3},{5,4},{6,5},{7,6},{8,7},{9,8},{10,9},{11,1... | collective-permute-start | bytes 552968 | tf_op jit(solution)/shard_map/ppermute | solution.py:681

commit v3 on v2

--- a/solution.py
+++ b/solution.py
@@ -59,12 +59,12 @@
 
 def take4(z):
     p03, m03, p12, m12 = z[0] + z[3], z[0] - z[3], z[1] + z[2], z[1] - z[2]
+    rest = p03 - p12
 
     def at(t, scale=1.0):
         b = [scale * x for x in cubic(t)]
-        even = p03 * (0.5 * (b[0] + b[3])) + p12 * (0.5 * (b[1] + b[2]))
-        odd = m03 * (0.5 * (b[0] - b[3])) + m12 * (0.5 * (b[1] - b[2]))
-        return even, odd
+        whole = p12 if scale == 1.0 else p12 * scale
+        return whole + rest * (b[0] + b[3]), m03 * (b[0] - b[3]) + m12 * (b[1] - b[2])
 
     return at
 
@@ -73,17 +73,17 @@
     p, m = d[0] + d[2], d[0] - d[2]
 
     def at(t, scale=1.0):
-        q = [scale * x for x in quadratic(t)]
+        q = [2.0 * scale * x for x in quadratic(t)]
         return p * (0.5 * (q[0] + q[2])) + d[1] * q[1], m * (0.5 * (q[0] - q[2]))
 
     return at
 
 
 def take2(g):
-    even, m = 0.5 * (g[0] + g[1]), g[0] - g[1]
+    even, m = g[0] + g[1], g[0] - g[1]
 
     def at(t):
-        return even, m * (0.5 - t)
+        return even, m * (1.0 - 2.0 * t)
 
     return at
 
@@ -97,18 +97,15 @@
 
 
 def put4(pairs, scale=1.0):
-    sums = None
+    total, sums = None, None
     for t, (one, two) in pairs:
         s, d = one + two, one - two
         b = [scale * x for x in cubic(t)]
-        terms = [
-            s * (0.5 * (b[0] + b[3])),
-            d * (0.5 * (b[0] - b[3])),
-            s * (0.5 * (b[1] + b[2])),
-            d * (0.5 * (b[1] - b[2])),
-        ]
+        total = s if total is None else total + s
+        terms = [s * (b[0] + b[3]), d * (b[0] - b[3]), d * (b[1] - b[2])]
         sums = terms if sums is None else [x + y for x, y in zip(sums, terms)]
-    e03, o03, e12, o12 = sums
+    e03, o03, o12 = sums
+    e12 = (total if scale == 1.0 else total * scale) - e03
     return [e03 + o03, e12 + o12, e12 - o12, e03 - o03]
 
 
@@ -116,7 +113,7 @@
     sums = None
     for t, (one, two) in pairs:
         s, d = one + two, one - two
-        q = quadratic(t)
+        q = [2.0 * x for x in quadratic(t)]
         terms = [s * (0.5 * (q[0] + q[2])), d * (0.5 * (q[0] - q[2])), s * q[1]]
         sums = terms if sums is None else [x + y for x, y in zip(sums, terms)]
     even, odd, middle = sums
@@ -126,10 +123,9 @@
 def put2(pairs):
     even, odd = None, None
     for t, (one, two) in pairs:
-        s, d = one + two, (one - two) * (0.5 - t)
+        s, d = one + two, (one - two) * (1.0 - 2.0 * t)
         even = s if even is None else even + s
         odd = d if odd is None else odd + d
-    even = 0.5 * even
     return [even + odd, even - odd]
 
 
@@ -151,8 +147,8 @@
     return body(rest, carry) if rest else carry
 
 
-def pack_kernel(own_cols, state_ref, direction_ref, thick_ref, column_ref, own_ref, head_ref, tail_ref):
-    length = thick_ref.shape[1]
+def pack_kernel(own_cols, fields_ref, column_ref, own_ref, head_ref, tail_ref):
+    length = fields_ref.shape[2]
     chunks = own_ref.shape[0] // (own_cols * SUBS)
     local = lax.rem(column_ref[0], own_cols).astype(jnp.float32)
 
@@ -168,13 +164,11 @@
                     row = (c * HALO + col - low) * SUBS + f
                     ref[row : row + 1, :] = part[col - rows : col - rows + 1]
 
-    sources = [(state_ref.at[i], i) for i in range(3)]
-    sources += [(direction_ref.at[i], 3 + i) for i in range(3)] + [(thick_ref, 6)]
     for rows in range(0, own_cols, SUBS):
-        for source, f in sources:
+        for f in range(7):
             for c in range(chunks):
                 width = min(LANES, length - c * LANES)
-                part = source[rows : rows + SUBS, c * LANES : c * LANES + width]
+                part = fields_ref[f, rows : rows + SUBS, c * LANES : c * LANES + width]
                 if width < LANES:
                     fill = jnp.zeros((SUBS, LANES - width), jnp.float32)
                     part = jnp.concatenate([part, fill], axis=1)
@@ -190,6 +184,8 @@
         self.sub = lax.broadcasted_iota(jnp.int32, (SUBS, LANES), 0)
         self.lane = lax.broadcasted_iota(jnp.int32, (SUBS, LANES), 1)
         self.low = self.sub < HALF
+        row = jnp.where(self.lane == 1, 4.0, jnp.where(self.lane < 3, 1.0, 0.0))
+        self.ends = jnp.where((self.sub == 0) | (self.sub == HALF), row, 0.0)
         self.zero = jnp.zeros((SUBS, LANES), jnp.float32)
         self.nothing = tuple((self.zero,) * 5 for _ in range(2))
         for h in range(2):
@@ -200,7 +196,7 @@
                 + [(1.0 - first, 1.0 - second), (first, second)]
             )
             for i, (x, y) in enumerate(rows):
-                table_ref[h, i] = jnp.where(self.low, jnp.float32(x), jnp.float32(y))
+                table_ref[h, i] = jnp.where(self.low, jnp.float32(0.5 * x), jnp.float32(0.5 * y))
 
     def spread(self, source, offset, count):
         for c in range(source.shape[0] // (count * SUBS)):
@@ -231,7 +227,7 @@
     def curve(self, g, h):
         return self.table_ref[h, 7] * g[0] + self.table_ref[h, 8] * g[1]
 
-    def axial_take(self, low, high, load, base, carry, thick=False, unroll=2):
+    def axial_take(self, low, high, load, base, carry, thick=False, unroll=4):
         take_ref = self.take_ref
 
         def differences(z):
@@ -408,14 +404,10 @@
         return stay + pltpu.roll(cross, 1, 0)
 
     def end_part(self, v):
-        corners = ((self.sub == 0) | (self.sub == HALF)) & (self.lane == 0)
-        row = (v + 4.0 * pltpu.roll(v, LANES - 1, 1) + pltpu.roll(v, LANES - 2, 1)) * (
-            END_STIFF / 36.0
-        )
-        row = jnp.where(corners, row, 0.0)
-        return row + 4.0 * pltpu.roll(row, 1, 1) + pltpu.roll(row, 2, 1)
-
-    def gather(self, low, high, load, image_ref, step, unroll=2):
+        total = jnp.sum(v * self.ends, axis=1, keepdims=True)
+        return (total * (END_STIFF / 36.0)) * self.ends
+
+    def gather(self, low, high, load, image_ref, step, unroll=4):
         acc_ref, halves = self.acc_ref, range(2)
 
         def back(name, col, h):
@@ -521,7 +513,7 @@
     for i, source in enumerate((left_ref, own_ref, right_ref)):
         column = jnp.max(source[7:8, :]).astype(jnp.int32)
         stringers.append(column + (pad + (i - 1) * own_cols))
-    marks = (1.0 / 6.0, 4.0 / 6.0, 1.0 / 6.0)
+    marks = (2.0 / 6.0, 8.0 / 6.0, 2.0 / 6.0)
 
     def line(name, column, h):
         return sum(marks[j] * take_ref[name, column + j, h] for j in range(3))
@@ -580,7 +572,7 @@
                     sums[n] = sums[n] + vectors[x] * vectors[y]
         return tuple(sums)
 
-    sums = loop(0, own_cols, inner, (zero,) * len(PAIRS))
+    sums = loop(0, own_cols, inner, (zero,) * len(PAIRS), 4)
     row = jnp.zeros((1, LANES), jnp.float32)
     for n, s in enumerate(sums):
         part = jnp.sum(jnp.sum(s, axis=0, keepdims=True), axis=1, keepdims=True)
@@ -665,6 +657,7 @@
     def params(mebibytes):
         return pltpu.CompilerParams(vmem_limit_bytes=mebibytes * 1024 * 1024)
 
+    fields = jnp.concatenate([state_field, direction, skin_thickness[None]], axis=0)
     packed, head, tail = pl.pallas_call(
         functools.partial(pack_kernel, own_cols),
         out_shape=(
@@ -672,11 +665,11 @@
             shape(chunks * HALO * SUBS, LANES),
             shape(chunks * HALO * SUBS, LANES),
         ),
-        in_specs=[vmem, vmem, vmem, smem],
+        in_specs=[vmem, smem],
         out_specs=(vmem,) * 3,
         compiler_params=params(8),
         name="pack",
-    )(state_field, direction, skin_thickness, stringer_column)
+    )(fields, stringer_column)
     left = lax.ppermute(tail, "circ", [(i, (i + 1) % count) for i in range(count)])
     right = lax.ppermute(head, "circ", [((i + 1) % count, i) for i in range(count)])
     buffers = (

time: 47.5 us -> 43 us (0.905)
  Pallas kernels: 27 us -> 23.5 us
  local copies, waits for them, and re-layouts: 2.57 us -> 0 us
  other arithmetic: 0 us -> 1.01 us
  blocking collectives: 10.7 us -> 11.4 us
    pallas_call x1, Pallas kernels: 20.7 us -> 17.9 us  [per_device(): pl.pallas_call(functools.partial(krylov_kernel, own_cols, pad, radius), o...]
    unnamed x6 -> x0, local copies, waits for them, and re-layouts: 2.57 us -> none
    concatenate x0 -> x1, other arithmetic: none -> 1.01 us  [per_device(): jnp.concatenate([state_field, direction, skin_thickness[None]], axis=0)]
    all_to_all x1, blocking collectives: 10.7 us -> 11.4 us  [per_device(): gram = lax.all_to_all(gram, 'circ', 0, 0, tiled=True)]
    pallas_call x1, Pallas kernels: 4.5 us -> 3.85 us  [per_device(): pl.pallas_call(functools.partial(own_kernel, own_cols, pad, radius), out_...]
  transfers between devices with their start and end apart: 2 -> 2, of which waited for: 0 -> 0; matrix products, arithmetic and copies ran while one was open for 0% -> 0% of each run, Pallas kernels for 10% -> 9%
where the time goes in v3:
time: 43 us; the launch traced here: 42.8 us
  Pallas kernels  23.5 us (55%)
  blocking collectives  11.4 us (27%)
  starting transfers between devices  5.59 us (13%)
  between operations  1.31 us (3%)
  other arithmetic  1.01 us (2%)
    pallas_call x1, Pallas kernels, per_device(): pl.pallas_call(functools.partial(krylov_kernel, own_cols, pad, radius), o...  17.9 us
    all_to_all x1, blocking collectives, per_device(): gram = lax.all_to_all(gram, 'circ', 0, 0, tiled=True)  11.4 us
    ppermute x1, starting transfers between devices, per_device(): lax.ppermute(head, 'circ', [((i + 1) % count, i) for i in range(count)])  5.05 us
    pallas_call x1, Pallas kernels, per_device(): pl.pallas_call(functools.partial(own_kernel, own_cols, pad, radius), out_...  3.85 us
    pallas_call x1, Pallas kernels, per_device(): pl.pallas_call(functools.partial(combine_kernel, count_all), out_shape=(s...  1.64 us
    concatenate x1, other arithmetic, per_device(): jnp.concatenate([state_field, direction, skin_thickness[None]], axis=0)  1.01 us
  transfers between devices with their start and end apart: 2, of which 0 were waited for; matrix products, arithmetic and copies ran while one was open for 0% of the time, Pallas kernels for 9%

profile of v3, /device:TPU:0, one launch (start us, length us, event | category | flops | bytes accessed | tf_op | source)
XLA Modules:
  0.0 42.8 jit_solution(17360782345089189460)
XLA Ops:
  1.3 1.0 %pad_maximum_fusion.fields_ref = f32[7,16,515]{2,1,0:T(8,128)S(1)} fusion(f32[1,16,515]{2,1,0:T(8,128)} %bitcast.7, f32[3,16,515]{2,1,0:T(8,128)} %param.5, f32[3,16,515]{2,1,0:T(8,128)} %param.4), kind=kLoop, calls=%fused_computation | loop fusion | flops 115360 | bytes 461440 | tf_op jit(solution)/shard_map/concatenate | solution.py:660
  2.3 0.1 pack.1
  2.4 0.5 %collective-permute-start = (f32[360,128]{1,0:T(8,128)S(1)}, f32[360,128]{1,0:T(8,128)S(1)}, u32[]{:S(2)}, u32[]{:S(2)}) collective-permute-start(f32[360,128]{1,0:T(8,128)S(1)} %get-tuple-element.13), channel_id=1, source_target_pairs={{0,1},{1,2},{2,3},{3,4},{4,5},{5,6},{6,7},{7,8},{8,9},{9,10},{10,1... | collective-permute-start | bytes 552968 | tf_op jit(solution)/shard_map/ppermute | solution.py:673
  3.0 5.0 %collective-permute-start.1 = (f32[360,128]{1,0:T(8,128)S(1)}, f32[360,128]{1,0:T(8,128)S(1)}, u32[]{:S(2)}, u32[]{:S(2)}) collective-permute-start(f32[360,128]{1,0:T(8,128)S(1)} %get-tuple-element.14), channel_id=1, source_target_pairs={{1,0},{2,1},{3,2},{4,3},{5,4},{6,5},{7,6},{8,7},{9,8},{10,9},{11,1... | collective-permute-start | bytes 552968 | tf_op jit(solution)/shard_map/ppermute | solution.py:674
  8.0 3.8 %own.1 = (f32[3072,128]{1,0:T(8,128)S(1)}, f32[21,48,2,8,128]{4,3,2,1,0:T(8,128)S(1)}, f32[10,48,2,8,128]{4,3,2,1,0:T(8,128)S(1)}, f32[48,2,4,8,8,128]{5,4,3,2,1,0:T(8,128)S(1)}, f32[2,2,5,8,128]{4,3,2,1,0:T(8,128)S(1)}) custom-call(f32[640,128]{1,0:T(8,128)S(1)} %get-tuple-element.15.own_ref), custom_call_target="tpu_custom_call" | custom-call | flops 40000000 | bytes 20000000 | tf_op jit(solution)/shard_map/own/pallas_call | solution.py:682
  11.9 0.0 collective-permute-done.left_ref
  11.9 0.0 collective-permute-done.1.right_ref
  11.9 17.9 %krylov.1 = (f32[4,384,128]{2,1,0:T(8,128)S(1)}, f32[16,128]{1,0:T(8,128)S(1)}, f32[3072,128]{1,0:T(8,128)S(1)}, f32[21,48,2,8,128]{4,3,2,1,0:T(8,128)S(1)}, f32...) custom-call(f32[360,128]{1,0:T(8,128)S(1)} %collective-permute-done., ...), custom_call_target="tpu_custom_call", output_to_operand_aliasing={{2}: (4, {}), {3}: (5, {}), {4}: (6, {}), {5}: (7, {})} | custom-call | tf_op jit(solution)/shard_map/krylov/pallas_call | solution.py:692
  29.8 11.4 %all_to_all.11 = f32[16,1,128]{2,1,0:T(1,128)S(1)} all-to-all(f32[16,1,128]{2,1,0:T(1,128)S(1)} %bitcast.6), channel_id=1, replica_groups=mesh['group'=2,'circ'=16] {'circ'}, dimensions={0} | all-to-all | bytes 16384 | tf_op jit(solution)/shard_map/all_to_all | solution.py:706
  41.2 1.6 %combine.1 = (f32[3,3,16,515]{3,2,1,0:T(8,128)}, f32[3]{0:T(128)}, f32[3]{0:T(128)}) custom-call(f32[16,128]{1,0:T(8,128)S(1)} %bitcast.5, f32[4,384,128]{2,1,0:T(8,128)S(1)} %get-tuple-element.22.krylov_ref), custom_call_target="tpu_custom_call" | custom-call | tf_op jit(solution)/shard_map/combine/pallas_call | solution.py:707
Async XLA Ops:
  2.4 9.4 %collective-permute-start = (f32[360,128]{1,0:T(8,128)S(1)}, f32[360,128]{1,0:T(8,128)S(1)}, u32[]{:S(2)}, u32[]{:S(2)}) collective-permute-start(f32[360,128]{1,0:T(8,128)S(1)} %get-tuple-element.13), channel_id=1, source_target_pairs={{0,1},{1,2},{2,3},{3,4},{4,5},{5,6},{6,7},{7,8},{8,9},{9,10},{10,1... | collective-permute-start | bytes 552968 | tf_op jit(solution)/shard_map/ppermute | solution.py:673
  3.0 8.9 %collective-permute-start.1 = (f32[360,128]{1,0:T(8,128)S(1)}, f32[360,128]{1,0:T(8,128)S(1)}, u32[]{:S(2)}, u32[]{:S(2)}) collective-permute-start(f32[360,128]{1,0:T(8,128)S(1)} %get-tuple-element.14), channel_id=1, source_target_pairs={{1,0},{2,1},{3,2},{4,3},{5,4},{6,5},{7,6},{8,7},{9,8},{10,9},{11,1... | collective-permute-start | bytes 552968 | tf_op jit(solution)/shard_map/ppermute | solution.py:674

commit v4 on v3

--- a/solution.py
+++ b/solution.py
@@ -130,6 +130,7 @@
 
 
 VECTOR = 11
+MARKS = (2.0 / 6.0, 8.0 / 6.0, 2.0 / 6.0)
 TAPS = ((F01, 4), (F00, 3), (F10, 3), (F11, 4), (F20, 4), (F20Q, 3), (F20L, 2), (F21, 4), (F21Q, 3), (F22, 4))
 PAIRS = [(i, j) for i in range(STEPS + 1) for j in range(i, STEPS + 1)]
 
@@ -407,6 +408,27 @@
         total = jnp.sum(v * self.ends, axis=1, keepdims=True)
         return (total * (END_STIFF / 36.0)) * self.ends
 
+    def line(self, name, column, h):
+        return sum(MARKS[j] * self.take_ref[name, column + j, h] for j in range(3))
+
+    def line_state(self, column, h):
+        along, tilt = self.line(A1, column, h), self.line(C1, column, h)
+        return along + 0.5 * tilt * tilt, tilt
+
+    def stringer(self, column, states):
+        for h in range(2):
+            weight = jnp.float32(WEIGHTS[h])
+            stretch, tilt = states[h]
+            slope_c = self.line(VECTOR + C1, column, h)
+            d_stretch = self.line(VECTOR + A1, column, h) + tilt * slope_c
+            f0 = (STRINGER_AXIAL * weight) * d_stretch
+            f1 = (STRINGER_AXIAL * weight) * (d_stretch * tilt + stretch * slope_c)
+            f2 = (STRINGER_BENDING * weight) * self.line(VECTOR + C2, column, h)
+            for j in range(3):
+                self.acc_ref[F01, column + j, h] += MARKS[j] * f0
+                self.acc_ref[F21, column + j, h] += MARKS[j] * f1
+                self.acc_ref[F22, column + j, h] += MARKS[j] * f2
+
     def gather(self, low, high, load, image_ref, step, unroll=4):
         acc_ref, halves = self.acc_ref, range(2)
 
@@ -449,7 +471,30 @@
         loop(low, high, body, 0, unroll)
 
 
-def own_kernel(own_cols, pad, radius, own_ref, field_ref, take_ref, acc_ref, state_ref, carry_ref, table_ref):
+def attached(source, shift):
+    return jnp.max(source[7:8, :]).astype(jnp.int32) + shift
+
+
+def keep(ref, index, carry):
+    for h in range(2):
+        for i in range(5):
+            ref[index, h, i] = carry[h][i]
+
+
+def own_kernel(
+    own_cols,
+    pad,
+    radius,
+    own_ref,
+    field_ref,
+    take_ref,
+    acc_ref,
+    second_ref,
+    state_ref,
+    image_ref,
+    carry_ref,
+    table_ref,
+):
     shell = Shell(own_cols, pad, radius, field_ref, take_ref, acc_ref, state_ref, table_ref)
     for col in range(pad, pad + own_cols):
         for i in range(3, 6):
@@ -457,17 +502,29 @@
             field_ref[start : start + SUBS, :] = shell.zero
     shell.spread(own_ref, pad, own_cols)
     stop = pad + own_cols
-    carry = shell.axial_take(pad, stop, lambda c, i: shell.field(c, (0, 1, 2, 6)[i]), 0, shell.nothing, thick=True)
-    for h in range(2):
-        for i in range(5):
-            carry_ref[0, h, i] = carry[h][i]
-    carry = shell.axial_take(pad, stop, lambda c, i: shell.field(c, 3 + i), VECTOR, shell.nothing)
-    for h in range(2):
-        for i in range(5):
-            carry_ref[1, h, i] = carry[h][i]
+
+    def state(col, index):
+        return shell.field(col, (0, 1, 2, 6)[index])
+
+    def direction(col, index):
+        return shell.field(col, 3 + index)
+
+    def image(col, index):
+        return image_ref[0, col, index]
+
+    keep(carry_ref, 0, shell.axial_take(pad, stop, state, 0, shell.nothing, thick=True))
+    keep(carry_ref, 1, shell.axial_take(pad, stop, direction, VECTOR, shell.nothing))
     shell.prepare(pad, stop - 3)
     shell.clear(pad)
     shell.spans(pad, stop - 3)
+    column = attached(own_ref, pad)
+    shell.stringer(column, [shell.line_state(column, h) for h in range(2)])
+    shell.gather(pad + 3, stop - 3, direction, image_ref, 0)
+
+    keep(carry_ref, 2, shell.axial_take(pad + 3, stop - 3, image, VECTOR, shell.nothing))
+    shell.acc_ref = second_ref
+    shell.clear(pad + 3)
+    shell.spans(pad + 3, stop - 6)
 
 
 def krylov_kernel(
@@ -481,12 +538,15 @@
     field_in,
     take_in,
     acc_in,
+    second_in,
     state_in,
+    image_in,
     krylov_ref,
     gram_ref,
     field_ref,
     take_ref,
     acc_ref,
+    second_ref,
     state_ref,
     image_ref,
     table_ref,
@@ -498,65 +558,63 @@
     shell.spread(left_ref, pad - HALO, HALO)
     shell.spread(right_ref, stop, HALO)
 
-    for index, base, names in ((0, 0, (0, 1, 2, 6)), (1, VECTOR, (3, 4, 5))):
-        def load(col, i, names=names):
-            return field(col, names[i])
-
-        thick = index == 0
-        shell.axial_take(pad - HALO, pad + 2, load, base, shell.nothing, thick=thick)
-        carry = tuple(tuple(carry_ref[index, h, i] for i in range(5)) for h in range(2))
-        shell.axial_take(stop, stop + HALO, load, base, carry, thick=thick)
+    def carried(index):
+        return tuple(tuple(carry_ref[index, h, i] for i in range(5)) for h in range(2))
+
+    def state(col, index):
+        return field(col, (0, 1, 2, 6)[index])
+
+    def vector(step):
+        def load(col, index):
+            if step == 0:
+                return field(col, 3 + index)
+            return image_ref[step - 1, col, index]
+
+        return load
+
+    shell.axial_take(pad - HALO, pad + 2, state, 0, shell.nothing, thick=True)
+    shell.axial_take(stop, stop + HALO, state, 0, carried(0), thick=True)
     shell.prepare(pad - HALO, pad)
     shell.prepare(stop - 3, stop + HALO - 3)
-
-    stringers = []
-    for i, source in enumerate((left_ref, own_ref, right_ref)):
-        column = jnp.max(source[7:8, :]).astype(jnp.int32)
-        stringers.append(column + (pad + (i - 1) * own_cols))
-    marks = (2.0 / 6.0, 8.0 / 6.0, 2.0 / 6.0)
-
-    def line(name, column, h):
-        return sum(marks[j] * take_ref[name, column + j, h] for j in range(3))
-
+    stringers = [
+        attached(source, pad + (i - 1) * own_cols)
+        for i, source in enumerate((left_ref, own_ref, right_ref))
+    ]
     for i, column in enumerate(stringers):
         for h in range(2):
-            along, tilt = line(A1, column, h), line(C1, column, h)
-            line_ref[i, h, 0] = along + 0.5 * tilt * tilt
-            line_ref[i, h, 1] = tilt
-
+            line_ref[i, h, 0], line_ref[i, h, 1] = shell.line_state(column, h)
+
+    def add_stringers(which):
+        for i in which:
+            shell.stringer(
+                stringers[i], [(line_ref[i, h, 0], line_ref[i, h, 1]) for h in range(2)]
+            )
+
+    low, high = pad, stop
     for step in range(STEPS):
         reach = HALO - 3 * step
         first, last = pad - reach, stop + reach - 3
-
-        def load(col, index, step=step):
-            if step == 0:
-                return field(col, 3 + index)
-            return image_ref[step - 1, col, index]
-
-        if step == 0:
-            shell.clear(first, reach)
-            shell.spans(first, pad, fresh=False)
-            shell.spans(stop - 3, last)
+        load = vector(step)
+        if step < 2:
+            shell.acc_ref = (acc_ref, second_ref)[step]
+            shell.axial_take(first, low + 2, load, VECTOR, shell.nothing)
+            shell.axial_take(high, last + 3, load, VECTOR, carried(1 + step))
+            shell.clear(first, low - first)
+            shell.spans(first, low, fresh=False)
+            shell.spans(high - 3, last)
+            low, high = low + 3, high - 3
         else:
+            shell.acc_ref = acc_ref
             shell.axial_take(first, last + 3, load, VECTOR, shell.nothing)
             shell.clear(first)
             shell.spans(first, last)
-
-        for i, column in enumerate(stringers):
-            for h in range(2):
-                weight = jnp.float32(WEIGHTS[h])
-                stretch, tilt = line_ref[i, h, 0], line_ref[i, h, 1]
-                slope_c = line(VECTOR + C1, column, h)
-                d_stretch = line(VECTOR + A1, column, h) + tilt * slope_c
-                f0 = (STRINGER_AXIAL * weight) * d_stretch
-                f1 = (STRINGER_AXIAL * weight) * (d_stretch * tilt + stretch * slope_c)
-                f2 = (STRINGER_BENDING * weight) * line(VECTOR + C2, column, h)
-                for j in range(3):
-                    acc_ref[F01, column + j, h] += marks[j] * f0
-                    acc_ref[F21, column + j, h] += marks[j] * f1
-                    acc_ref[F22, column + j, h] += marks[j] * f2
-
-        shell.gather(first + 3, last, load, image_ref, step)
+        if step == 0:
+            add_stringers((0, 2))
+            shell.gather(first + 3, low, load, image_ref, step)
+            shell.gather(high, last, load, image_ref, step)
+        else:
+            add_stringers(range(3))
+            shell.gather(first + 3, last, load, image_ref, step)
 
     def inner(cols, sums):
         sums = list(sums)
@@ -676,14 +734,16 @@
         shape(columns * SUBS * SUBS, LANES),
         shape(21, columns, 2, SUBS, LANES),
         shape(10, columns, 2, SUBS, LANES),
+        shape(10, columns, 2, SUBS, LANES),
         shape(columns, 2, 4, 8, SUBS, LANES),
+        shape(STEPS, columns, 3, SUBS, LANES),
     )
     table = pltpu.VMEM((2, 9, SUBS, LANES), jnp.float32)
     *kept, carry = pl.pallas_call(
         functools.partial(own_kernel, own_cols, pad, radius),
-        out_shape=buffers + (shape(2, 2, 5, SUBS, LANES),),
+        out_shape=buffers + (shape(3, 2, 5, SUBS, LANES),),
         in_specs=[vmem],
-        out_specs=(vmem,) * 5,
+        out_specs=(vmem,) * 7,
         scratch_shapes=[table],
         compiler_params=params(4),
         cost_estimate=pl.CostEstimate(flops=40000000, bytes_accessed=20000000, transcendentals=0),
@@ -692,11 +752,10 @@
     krylov, gram, *_ = pl.pallas_call(
         functools.partial(krylov_kernel, own_cols, pad, radius),
         out_shape=(shape(STEPS + 1, own_cols * 3 * SUBS, LANES), shape(count, LANES)) + buffers,
-        in_specs=[vmem] * 8,
-        out_specs=(vmem,) * 6,
-        input_output_aliases={4: 2, 5: 3, 6: 4, 7: 5},
+        in_specs=[vmem] * 10,
+        out_specs=(vmem,) * 8,
+        input_output_aliases={4 + i: 2 + i for i in range(len(buffers))},
         scratch_shapes=[
-            pltpu.VMEM((STEPS, columns, 3, SUBS, LANES), jnp.float32),
             table,
             pltpu.VMEM((3, 2, 2, SUBS, LANES), jnp.float32),
         ],

time: 43 us -> 41.9 us (0.974)
  blocking collectives: 11.4 us -> 9.85 us
    pallas_call x1, Pallas kernels: 3.85 us -> 6 us  [per_device(): pl.pallas_call(functools.partial(own_kernel, own_cols, pad, radius), out_...]
    pallas_call x1, Pallas kernels: 17.9 us -> 16.2 us  [per_device(): pl.pallas_call(functools.partial(krylov_kernel, own_cols, pad, radius), o...]
    all_to_all x1, blocking collectives: 11.4 us -> 9.85 us  [per_device(): gram = lax.all_to_all(gram, 'circ', 0, 0, tiled=True)]
  transfers between devices with their start and end apart: 2 -> 2, of which waited for: 0 -> 0; matrix products, arithmetic and copies ran while one was open for 0% -> 0% of each run, Pallas kernels for 9% -> 14%
where the time goes in v4:
time: 41.9 us; the launch traced here: 41.7 us
  Pallas kernels  23.9 us (57%)
  blocking collectives  9.85 us (24%)
  starting transfers between devices  5.59 us (13%)
  between operations  1.31 us (3%)
  other arithmetic  1.01 us (2%)
    pallas_call x1, Pallas kernels, per_device(): pl.pallas_call(functools.partial(krylov_kernel, own_cols, pad, radius), o...  16.2 us
    all_to_all x1, blocking collectives, per_device(): gram = lax.all_to_all(gram, 'circ', 0, 0, tiled=True)  9.85 us
    pallas_call x1, Pallas kernels, per_device(): pl.pallas_call(functools.partial(own_kernel, own_cols, pad, radius), out_...  6 us
    ppermute x1, starting transfers between devices, per_device(): lax.ppermute(head, 'circ', [((i + 1) % count, i) for i in range(count)])  5.05 us
    pallas_call x1, Pallas kernels, per_device(): pl.pallas_call(functools.partial(combine_kernel, count_all), out_shape=(s...  1.64 us
    concatenate x1, other arithmetic, per_device(): jnp.concatenate([state_field, direction, skin_thickness[None]], axis=0)  1.01 us
  transfers between devices with their start and end apart: 2, of which 0 were waited for; matrix products, arithmetic and copies ran while one was open for 0% of the time, Pallas kernels for 14%

profile of v4, /device:TPU:0, one launch (start us, length us, event | category | flops | bytes accessed | tf_op | source)
XLA Modules:
  0.0 41.7 jit_solution(8008446271210518339)
XLA Ops:
  1.3 1.0 %pad_maximum_fusion.fields_ref = f32[7,16,515]{2,1,0:T(8,128)S(1)} fusion(f32[1,16,515]{2,1,0:T(8,128)} %bitcast.7, f32[3,16,515]{2,1,0:T(8,128)} %param.5, f32[3,16,515]{2,1,0:T(8,128)} %param.4), kind=kLoop, calls=%fused_computation | loop fusion | flops 115360 | bytes 461440 | tf_op jit(solution)/shard_map/concatenate | solution.py:718
  2.3 0.1 pack.1
  2.4 0.5 %collective-permute-start = (f32[360,128]{1,0:T(8,128)S(1)}, f32[360,128]{1,0:T(8,128)S(1)}, u32[]{:S(2)}, u32[]{:S(2)}) collective-permute-start(f32[360,128]{1,0:T(8,128)S(1)} %get-tuple-element.15), channel_id=1, source_target_pairs={{0,1},{1,2},{2,3},{3,4},{4,5},{5,6},{6,7},{7,8},{8,9},{9,10},{10,1... | collective-permute-start | bytes 552968 | tf_op jit(solution)/shard_map/ppermute | solution.py:731
  3.0 5.0 %collective-permute-start.1 = (f32[360,128]{1,0:T(8,128)S(1)}, f32[360,128]{1,0:T(8,128)S(1)}, u32[]{:S(2)}, u32[]{:S(2)}) collective-permute-start(f32[360,128]{1,0:T(8,128)S(1)} %get-tuple-element.16), channel_id=1, source_target_pairs={{1,0},{2,1},{3,2},{4,3},{5,4},{6,5},{7,6},{8,7},{9,8},{10,9},{11,1... | collective-permute-start | bytes 552968 | tf_op jit(solution)/shard_map/ppermute | solution.py:732
  8.0 6.0 %own.1 = (f32[3072,128]{1,0:T(8,128)S(1)}, f32[21,48,2,8,128]{4,3,2,1,0:T(8,128)S(1)}, f32[10,48,2,8,128]{4,3,2,1,0:T(8,128)S(1)}, f32[10,48,2,8,128]{4,3,2,1,0:...) custom-call(f32[640,128]{1,0:T(8,128)S(1)} %get-tuple-element.17.own_ref), custom_call_target="tpu_custom_call" | custom-call | flops 40000000 | bytes 20000000 | tf_op jit(solution)/shard_map/own/pallas_call | solution.py:742
  14.0 0.0 collective-permute-done.left_ref
  14.0 0.0 collective-permute-done.1.right_ref
  14.1 16.2 %krylov.1 = (f32[4,384,128]{2,1,0:T(8,128)S(1)}, f32[16,128]{1,0:T(8,128)S(1)}, f32[3072,128]{1,0:T(8,128)S(1)}, f32[21,48,2,8,128]{4,3,2,1,0:T(8,128)S(1)}, f32...) custom-call(f32[360,128]{1,0:T(8,128)S(1)} %collective-permute-done., ...), custom_call_target="tpu_custom_call", output_to_operand_aliasing={{2}: (4, {}), {3}: (5, {}), {4}: (6, {}), {5}: (7, {}), {6}... | custom-call | tf_op jit(solution)/shard_map/krylov/pallas_call | solution.py:752
  30.2 9.9 %all_to_all.11 = f32[16,1,128]{2,1,0:T(1,128)S(1)} all-to-all(f32[16,1,128]{2,1,0:T(1,128)S(1)} %bitcast.6), channel_id=1, replica_groups=mesh['group'=2,'circ'=16] {'circ'}, dimensions={0} | all-to-all | bytes 16384 | tf_op jit(solution)/shard_map/all_to_all | solution.py:765
  40.1 1.6 %combine.1 = (f32[3,3,16,515]{3,2,1,0:T(8,128)}, f32[3]{0:T(128)}, f32[3]{0:T(128)}) custom-call(f32[16,128]{1,0:T(8,128)S(1)} %bitcast.5, f32[4,384,128]{2,1,0:T(8,128)S(1)} %get-tuple-element.26.krylov_ref), custom_call_target="tpu_custom_call" | custom-call | tf_op jit(solution)/shard_map/combine/pallas_call | solution.py:766
Async XLA Ops:
  2.4 11.6 %collective-permute-start = (f32[360,128]{1,0:T(8,128)S(1)}, f32[360,128]{1,0:T(8,128)S(1)}, u32[]{:S(2)}, u32[]{:S(2)}) collective-permute-start(f32[360,128]{1,0:T(8,128)S(1)} %get-tuple-element.15), channel_id=1, source_target_pairs={{0,1},{1,2},{2,3},{3,4},{4,5},{5,6},{6,7},{7,8},{8,9},{9,10},{10,1... | collective-permute-start | bytes 552968 | tf_op jit(solution)/shard_map/ppermute | solution.py:731
  3.0 11.1 %collective-permute-start.1 = (f32[360,128]{1,0:T(8,128)S(1)}, f32[360,128]{1,0:T(8,128)S(1)}, u32[]{:S(2)}, u32[]{:S(2)}) collective-permute-start(f32[360,128]{1,0:T(8,128)S(1)} %get-tuple-element.16), channel_id=1, source_target_pairs={{1,0},{2,1},{3,2},{4,3},{5,4},{6,5},{7,6},{8,7},{9,8},{10,9},{11,1... | collective-permute-start | bytes 552968 | tf_op jit(solution)/shard_map/ppermute | solution.py:732

commit v5 on v4

--- a/solution.py
+++ b/solution.py
@@ -228,40 +228,43 @@
     def curve(self, g, h):
         return self.table_ref[h, 7] * g[0] + self.table_ref[h, 8] * g[1]
 
-    def axial_take(self, low, high, load, base, carry, thick=False, unroll=4):
+    def take_columns(self, cols, load, base, carry, thick=False):
         take_ref = self.take_ref
 
         def differences(z):
             return [z[o + 1] - z[o] for o in range(len(z) - 1)]
 
+        loaded = [[load(col, i) for i in range(4 if thick else 3)] for col in cols]
+        for col, vectors in zip(cols, loaded):
+            za, zb, zc = (self.shifted(v) for v in vectors[:3])
+            da, db, dc = differences(za), differences(zb), differences(zc)
+            gc = differences(dc)
+            zh = self.shifted(vectors[3]) if thick else None
+            out = []
+            for h in range(2):
+                old_a0, old_b0, old_c0, old_c1, old_dc0 = carry[h]
+                a0, b0, c0 = self.value(za, h), self.value(zb, h), self.value(zc, h)
+                c1, dc0 = self.slope(dc, h), c0 - old_c0
+                take_ref[base + A1, col, h] = self.slope(da, h)
+                take_ref[base + B1, col, h] = self.slope(db, h)
+                take_ref[base + C0, col, h] = c0
+                take_ref[base + C1, col, h] = c1
+                take_ref[base + DA0, col - 1, h] = a0 - old_a0
+                take_ref[base + DB0, col - 1, h] = b0 - old_b0
+                take_ref[base + DC0, col - 1, h] = dc0
+                if thick:
+                    take_ref[base + H0, col, h] = self.value(zh, h)
+                else:
+                    take_ref[base + C2, col, h] = self.curve(gc, h)
+                    take_ref[base + DC1, col - 1, h] = c1 - old_c1
+                    take_ref[base + DDC0, col - 2, h] = dc0 - old_dc0
+                out.append((a0, b0, c0, c1, dc0))
+            carry = tuple(out)
+        return carry
+
+    def axial_take(self, low, high, load, base, carry, thick=False, unroll=4):
         def body(cols, carry):
-            loaded = [[load(col, i) for i in range(4 if thick else 3)] for col in cols]
-            for col, vectors in zip(cols, loaded):
-                za, zb, zc = (self.shifted(v) for v in vectors[:3])
-                da, db, dc = differences(za), differences(zb), differences(zc)
-                gc = differences(dc)
-                zh = self.shifted(vectors[3]) if thick else None
-                out = []
-                for h in range(2):
-                    old_a0, old_b0, old_c0, old_c1, old_dc0 = carry[h]
-                    a0, b0, c0 = self.value(za, h), self.value(zb, h), self.value(zc, h)
-                    c1, dc0 = self.slope(dc, h), c0 - old_c0
-                    take_ref[base + A1, col, h] = self.slope(da, h)
-                    take_ref[base + B1, col, h] = self.slope(db, h)
-                    take_ref[base + C0, col, h] = c0
-                    take_ref[base + C1, col, h] = c1
-                    take_ref[base + DA0, col - 1, h] = a0 - old_a0
-                    take_ref[base + DB0, col - 1, h] = b0 - old_b0
-                    take_ref[base + DC0, col - 1, h] = dc0
-                    if thick:
-                        take_ref[base + H0, col, h] = self.value(zh, h)
-                    else:
-                        take_ref[base + C2, col, h] = self.curve(gc, h)
-                        take_ref[base + DC1, col - 1, h] = c1 - old_c1
-                        take_ref[base + DDC0, col - 2, h] = dc0 - old_dc0
-                    out.append((a0, b0, c0, c1, dc0))
-                carry = tuple(out)
-            return carry
+            return self.take_columns(cols, load, base, carry, thick)
 
         return loop(low, high, body, carry, unroll)
 
@@ -429,46 +432,62 @@
                 self.acc_ref[F21, column + j, h] += MARKS[j] * f1
                 self.acc_ref[F22, column + j, h] += MARKS[j] * f2
 
-    def gather(self, low, high, load, image_ref, step, unroll=4):
+    def image_columns(self, cols, load):
         acc_ref, halves = self.acc_ref, range(2)
 
         def back(name, col, h):
             return acc_ref[name, col - 1, h] - acc_ref[name, col, h]
 
-        def body(cols, unused):
-            work = []
-            for col in cols:
-                zeroth = [
-                    [back(F00, col, h) for h in halves],
-                    [back(F10, col, h) for h in halves],
-                    [
-                        acc_ref[F20, col, h]
-                        + back(F20Q, col, h)
-                        + (acc_ref[F20L, col - 2, h] - acc_ref[F20L, col - 1, h])
-                        - back(F20L, col, h)
-                        for h in halves
-                    ],
-                ]
-                first = [
-                    [acc_ref[F01, col, h] for h in halves],
-                    [acc_ref[F11, col, h] for h in halves],
-                    [acc_ref[F21, col, h] + back(F21Q, col, h) for h in halves],
-                ]
-                second = [None, None, [acc_ref[F22, col, h] for h in halves]]
-                work.append((zeroth, first, second, [load(col, i) for i in range(3)]))
-            images = [
+        work = []
+        for col in cols:
+            zeroth = [
+                [back(F00, col, h) for h in halves],
+                [back(F10, col, h) for h in halves],
                 [
-                    self.axial_put(zeroth[i], first[i], second[i]) + self.end_part(v[i])
-                    for i in range(3)
-                ]
-                for zeroth, first, second, v in work
+                    acc_ref[F20, col, h]
+                    + back(F20Q, col, h)
+                    + (acc_ref[F20L, col - 2, h] - acc_ref[F20L, col - 1, h])
+                    - back(F20L, col, h)
+                    for h in halves
+                ],
             ]
+            first = [
+                [acc_ref[F01, col, h] for h in halves],
+                [acc_ref[F11, col, h] for h in halves],
+                [acc_ref[F21, col, h] + back(F21Q, col, h) for h in halves],
+            ]
+            second = [None, None, [acc_ref[F22, col, h] for h in halves]]
+            work.append((zeroth, first, second, [load(col, i) for i in range(3)]))
+        return [
+            [
+                self.axial_put(zeroth[i], first[i], second[i]) + self.end_part(v[i])
+                for i in range(3)
+            ]
+            for zeroth, first, second, v in work
+        ]
+
+    def gather(self, low, high, load, image_ref, step, follow, carry, unroll, beyond=0):
+        count = high - low
+        ahead = min(count, unroll + count % unroll)
+
+        def put(cols, images):
             for col, image in zip(cols, images):
                 for i in range(3):
                     image_ref[step, col, i] = image[i]
-            return unused
-
-        loop(low, high, body, 0, unroll)
+
+        def body(start, carry):
+            cols = [start + ahead + u for u in range(unroll)]
+            images = self.image_columns(cols, load)
+            carry = follow([start + u for u in range(unroll)], carry)
+            put(cols, images)
+            return carry
+
+        cols = list(range(low, low + ahead))
+        put(cols, self.image_columns(cols, load))
+        rounds = (count - ahead) // unroll
+        if rounds > 0:
+            carry = lax.fori_loop(0, rounds, lambda i, c: body(low + i * unroll, c), carry)
+        return follow(list(range(low + rounds * unroll, high + beyond)), carry)
 
 
 def attached(source, shift):
@@ -519,9 +538,14 @@
     shell.spans(pad, stop - 3)
     column = attached(own_ref, pad)
     shell.stringer(column, [shell.line_state(column, h) for h in range(2)])
-    shell.gather(pad + 3, stop - 3, direction, image_ref, 0)
-
-    keep(carry_ref, 2, shell.axial_take(pad + 3, stop - 3, image, VECTOR, shell.nothing))
+
+    def follow(cols, carry):
+        return shell.take_columns(cols, image, VECTOR, carry)
+
+    carry = shell.gather(
+        pad + 3, stop - 3, direction, image_ref, 0, follow, shell.nothing, unroll=3
+    )
+    keep(carry_ref, 2, carry)
     shell.acc_ref = second_ref
     shell.clear(pad + 3)
     shell.spans(pad + 3, stop - 6)
@@ -590,47 +614,54 @@
                 stringers[i], [(line_ref[i, h, 0], line_ref[i, h, 1]) for h in range(2)]
             )
 
-    low, high = pad, stop
-    for step in range(STEPS):
-        reach = HALO - 3 * step
-        first, last = pad - reach, stop + reach - 3
-        load = vector(step)
-        if step < 2:
-            shell.acc_ref = (acc_ref, second_ref)[step]
-            shell.axial_take(first, low + 2, load, VECTOR, shell.nothing)
-            shell.axial_take(high, last + 3, load, VECTOR, carried(1 + step))
-            shell.clear(first, low - first)
-            shell.spans(first, low, fresh=False)
-            shell.spans(high - 3, last)
-            low, high = low + 3, high - 3
-        else:
-            shell.acc_ref = acc_ref
-            shell.axial_take(first, last + 3, load, VECTOR, shell.nothing)
-            shell.clear(first)
-            shell.spans(first, last)
-        if step == 0:
-            add_stringers((0, 2))
-            shell.gather(first + 3, low, load, image_ref, step)
-            shell.gather(high, last, load, image_ref, step)
-        else:
-            add_stringers(range(3))
-            shell.gather(first + 3, last, load, image_ref, step)
+    def take_next(step):
+        load = vector(step + 1)
+        return lambda cols, carry: shell.take_columns(cols, load, VECTOR, carry)
 
     def inner(cols, sums):
         sums = list(sums)
         for col in cols:
             for comp in range(3):
-                vectors = [field(pad + col, 3 + comp)] + [
-                    image_ref[s, pad + col, comp] for s in range(STEPS)
-                ]
-                for s, vector in enumerate(vectors):
-                    start = pl.multiple_of(col * (3 * SUBS) + comp * SUBS, SUBS)
-                    krylov_ref[s, pl.ds(start, SUBS), :] = vector
-                for n, (x, y) in enumerate(PAIRS):
-                    sums[n] = sums[n] + vectors[x] * vectors[y]
+                vectors = [vector(s)(col, comp) for s in range(STEPS + 1)]
+                for s, x in enumerate(vectors):
+                    start = (col - pad) * (3 * SUBS) + comp * SUBS
+                    if not isinstance(start, int):
+                        start = pl.multiple_of(start, SUBS)
+                    krylov_ref[s, pl.ds(start, SUBS), :] = x
+                for n, (i, j) in enumerate(PAIRS):
+                    sums[n] = sums[n] + vectors[i] * vectors[j]
         return tuple(sums)
 
-    sums = loop(0, own_cols, inner, (zero,) * len(PAIRS), 4)
+    for step in range(STEPS):
+        reach = HALO - 3 * step
+        first, last = pad - reach, stop + reach - 3
+        low, high = pad + 3 * step, stop - 3 * step
+        load = vector(step)
+        if step == 0:
+            shell.axial_take(first, low + 2, load, VECTOR, shell.nothing)
+            shell.axial_take(high, last + 3, load, VECTOR, carried(1))
+        shell.acc_ref = second_ref if step == 1 else acc_ref
+        if step < 2:
+            shell.clear(first, low - first)
+            shell.spans(first, low, fresh=False)
+            shell.spans(high - 3, last)
+        else:
+            shell.clear(first)
+            shell.spans(first, last)
+        add_stringers((0, 2) if step == 0 else (0, 1, 2))
+        if step == 0:
+            follow = take_next(step)
+            shell.gather(
+                first + 3, low + 3, load, image_ref, step, follow, shell.nothing, 3, beyond=2
+            )
+            shell.gather(high - 3, last, load, image_ref, step, follow, carried(2), 3)
+        elif step < STEPS - 1:
+            follow = take_next(step)
+            shell.gather(first + 3, last, load, image_ref, step, follow, shell.nothing, 4)
+        else:
+            nothing = (zero,) * len(PAIRS)
+            sums = shell.gather(pad, stop, load, image_ref, step, inner, nothing, 4)
+
     row = jnp.zeros((1, LANES), jnp.float32)
     for n, s in enumerate(sums):
         part = jnp.sum(jnp.sum(s, axis=0, keepdims=True), axis=1, keepdims=True)

time: 41.9 us -> 40.9 us (0.976)
  Pallas kernels: 23.9 us -> 23 us
    pallas_call x1, Pallas kernels: 16.2 us -> 15.4 us  [per_device(): pl.pallas_call(functools.partial(krylov_kernel, own_cols, pad, radius), o...]
where the time goes in v5:
time: 40.9 us; the launch traced here: 40.7 us
  Pallas kernels  23 us (56%)
  blocking collectives  9.86 us (24%)
  starting transfers between devices  5.59 us (14%)
  between operations  1.31 us (3%)
  other arithmetic  1.01 us (2%)
    pallas_call x1, Pallas kernels, per_device(): pl.pallas_call(functools.partial(krylov_kernel, own_cols, pad, radius), o...  15.4 us
    all_to_all x1, blocking collectives, per_device(): gram = lax.all_to_all(gram, 'circ', 0, 0, tiled=True)  9.86 us
    pallas_call x1, Pallas kernels, per_device(): pl.pallas_call(functools.partial(own_kernel, own_cols, pad, radius), out_...  5.78 us
    ppermute x1, starting transfers between devices, per_device(): lax.ppermute(head, 'circ', [((i + 1) % count, i) for i in range(count)])  5.05 us
    pallas_call x1, Pallas kernels, per_device(): pl.pallas_call(functools.partial(combine_kernel, count_all), out_shape=(s...  1.64 us
    concatenate x1, other arithmetic, per_device(): jnp.concatenate([state_field, direction, skin_thickness[None]], axis=0)  1.01 us
  transfers between devices with their start and end apart: 2, of which 0 were waited for; matrix products, arithmetic and copies ran while one was open for 0% of the time, Pallas kernels for 14%

profile of v5, /device:TPU:0, one launch (start us, length us, event | category | flops | bytes accessed | tf_op | source)
XLA Modules:
  0.0 40.7 jit_solution(10787733881695827783)
XLA Ops:
  1.3 1.0 %pad_maximum_fusion.fields_ref = f32[7,16,515]{2,1,0:T(8,128)S(1)} fusion(f32[1,16,515]{2,1,0:T(8,128)} %bitcast.7, f32[3,16,515]{2,1,0:T(8,128)} %param.5, f32[3,16,515]{2,1,0:T(8,128)} %param.4), kind=kLoop, calls=%fused_computation | loop fusion | flops 115360 | bytes 461440 | tf_op jit(solution)/shard_map/concatenate | solution.py:749
  2.3 0.1 pack.1
  2.4 0.5 %collective-permute-start = (f32[360,128]{1,0:T(8,128)S(1)}, f32[360,128]{1,0:T(8,128)S(1)}, u32[]{:S(2)}, u32[]{:S(2)}) collective-permute-start(f32[360,128]{1,0:T(8,128)S(1)} %get-tuple-element.15), channel_id=1, source_target_pairs={{0,1},{1,2},{2,3},{3,4},{4,5},{5,6},{6,7},{7,8},{8,9},{9,10},{10,1... | collective-permute-start | bytes 552968 | tf_op jit(solution)/shard_map/ppermute | solution.py:762
  3.0 5.0 %collective-permute-start.1 = (f32[360,128]{1,0:T(8,128)S(1)}, f32[360,128]{1,0:T(8,128)S(1)}, u32[]{:S(2)}, u32[]{:S(2)}) collective-permute-start(f32[360,128]{1,0:T(8,128)S(1)} %get-tuple-element.16), channel_id=1, source_target_pairs={{1,0},{2,1},{3,2},{4,3},{5,4},{6,5},{7,6},{8,7},{9,8},{10,9},{11,1... | collective-permute-start | bytes 552968 | tf_op jit(solution)/shard_map/ppermute | solution.py:763
  8.0 5.8 %own.1 = (f32[3072,128]{1,0:T(8,128)S(1)}, f32[21,48,2,8,128]{4,3,2,1,0:T(8,128)S(1)}, f32[10,48,2,8,128]{4,3,2,1,0:T(8,128)S(1)}, f32[10,48,2,8,128]{4,3,2,1,0:...) custom-call(f32[640,128]{1,0:T(8,128)S(1)} %get-tuple-element.17.own_ref), custom_call_target="tpu_custom_call" | custom-call | flops 40000000 | bytes 20000000 | tf_op jit(solution)/shard_map/own/pallas_call | solution.py:773
  13.8 0.0 collective-permute-done.left_ref
  13.8 0.0 collective-permute-done.1.right_ref
  13.8 15.4 %krylov.1 = (f32[4,384,128]{2,1,0:T(8,128)S(1)}, f32[16,128]{1,0:T(8,128)S(1)}, f32[3072,128]{1,0:T(8,128)S(1)}, f32[21,48,2,8,128]{4,3,2,1,0:T(8,128)S(1)}, f32...) custom-call(f32[360,128]{1,0:T(8,128)S(1)} %collective-permute-done., ...), custom_call_target="tpu_custom_call", output_to_operand_aliasing={{2}: (4, {}), {3}: (5, {}), {4}: (6, {}), {5}: (7, {}), {6}... | custom-call | tf_op jit(solution)/shard_map/krylov/pallas_call | solution.py:783
  29.2 9.9 %all_to_all.11 = f32[16,1,128]{2,1,0:T(1,128)S(1)} all-to-all(f32[16,1,128]{2,1,0:T(1,128)S(1)} %bitcast.6), channel_id=1, replica_groups=mesh['group'=2,'circ'=16] {'circ'}, dimensions={0} | all-to-all | bytes 16384 | tf_op jit(solution)/shard_map/all_to_all | solution.py:796
  39.1 1.6 %combine.1 = (f32[3,3,16,515]{3,2,1,0:T(8,128)}, f32[3]{0:T(128)}, f32[3]{0:T(128)}) custom-call(f32[16,128]{1,0:T(8,128)S(1)} %bitcast.5, f32[4,384,128]{2,1,0:T(8,128)S(1)} %get-tuple-element.26.krylov_ref), custom_call_target="tpu_custom_call" | custom-call | tf_op jit(solution)/shard_map/combine/pallas_call | solution.py:797
Async XLA Ops:
  2.4 11.4 %collective-permute-start = (f32[360,128]{1,0:T(8,128)S(1)}, f32[360,128]{1,0:T(8,128)S(1)}, u32[]{:S(2)}, u32[]{:S(2)}) collective-permute-start(f32[360,128]{1,0:T(8,128)S(1)} %get-tuple-element.15), channel_id=1, source_target_pairs={{0,1},{1,2},{2,3},{3,4},{4,5},{5,6},{6,7},{7,8},{8,9},{9,10},{10,1... | collective-permute-start | bytes 552968 | tf_op jit(solution)/shard_map/ppermute | solution.py:762
  3.0 10.8 %collective-permute-start.1 = (f32[360,128]{1,0:T(8,128)S(1)}, f32[360,128]{1,0:T(8,128)S(1)}, u32[]{:S(2)}, u32[]{:S(2)}) collective-permute-start(f32[360,128]{1,0:T(8,128)S(1)} %get-tuple-element.16), channel_id=1, source_target_pairs={{1,0},{2,1},{3,2},{4,3},{5,4},{6,5},{7,6},{8,7},{9,8},{10,9},{11,1... | collective-permute-start | bytes 552968 | tf_op jit(solution)/shard_map/ppermute | solution.py:763

commit v6 on v5

--- a/solution.py
+++ b/solution.py
@@ -148,13 +148,19 @@
     return body(rest, carry) if rest else carry
 
 
+REST, FIRST_REST, ABOVE = 3, 24, 64
+
+
 def pack_kernel(own_cols, fields_ref, column_ref, own_ref, head_ref, tail_ref):
     length = fields_ref.shape[2]
     chunks = own_ref.shape[0] // (own_cols * SUBS)
     local = lax.rem(column_ref[0], own_cols).astype(jnp.float32)
+    lane = lax.broadcasted_iota(jnp.int32, (SUBS, LANES), 1)
 
     def put(f, rows, part, c):
         own_ref[pl.ds((c * own_cols + rows) * SUBS + f, SUBS, stride=SUBS), :] = part
+        if c == chunks - 1:
+            return
         for ref, low in ((head_ref, 0), (tail_ref, own_cols - HALO)):
             start, stop = max(rows, low), min(rows + SUBS, low + HALO)
             if stop - start == SUBS:
@@ -166,6 +172,7 @@
                     ref[row : row + 1, :] = part[col - rows : col - rows + 1]
 
     for rows in range(0, own_cols, SUBS):
+        rests = jnp.where(lane < ABOVE, 0.0, local)
         for f in range(7):
             for c in range(chunks):
                 width = min(LANES, length - c * LANES)
@@ -173,8 +180,9 @@
                 if width < LANES:
                     fill = jnp.zeros((SUBS, LANES - width), jnp.float32)
                     part = jnp.concatenate([part, fill], axis=1)
+                    rests = rests + pltpu.roll(part, FIRST_REST - REST * f, 1)
                 put(f, rows, part, c)
-        put(7, rows, jnp.full((SUBS, LANES), local), 0)
+        put(7, rows, rests, 0)
 
 
 class Shell:
@@ -187,6 +195,7 @@
         self.low = self.sub < HALF
         row = jnp.where(self.lane == 1, 4.0, jnp.where(self.lane < 3, 1.0, 0.0))
         self.ends = jnp.where((self.sub == 0) | (self.sub == HALF), row, 0.0)
+        self.springs = self.ends * (END_STIFF / 36.0)
         self.zero = jnp.zeros((SUBS, LANES), jnp.float32)
         self.nothing = tuple((self.zero,) * 5 for _ in range(2))
         for h in range(2):
@@ -205,6 +214,16 @@
                 start = (offset + i) * SUBS * SUBS + c
                 row = (c * count + i) * SUBS
                 self.field_ref[pl.ds(start, SUBS, stride=SUBS), :] = source[row : row + SUBS, :]
+
+    def spread_rests(self, source, offset, count):
+        chunk = source.shape[0] // (count * SUBS)
+        for i in range(count):
+            row = jnp.broadcast_to(source[i * SUBS + 7 : i * SUBS + 8, :], (SUBS, LANES))
+            rests = pltpu.roll(row, LANES - FIRST_REST, 1, stride=REST, stride_axis=0)
+            start = (offset + i) * SUBS * SUBS + chunk
+            self.field_ref[pl.ds(start, SUBS, stride=SUBS), :] = jnp.where(
+                self.lane < REST, rests, 0.0
+            )
 
     def field(self, col, index):
         start = col * (SUBS * SUBS) + index * SUBS
@@ -398,18 +417,45 @@
         if second is not None:
             l0, l1 = (sum(table_ref[h, 7 + o] * second[h] for h in range(2)) for o in range(2))
             t = [t[0] + l0, t[1] + (l1 - 2.0 * l0), t[2] + (l0 - 2.0 * l1), t[3] + l1]
-        stay, cross = t[0], self.zero
-        for o in range(1, 4):
-            moved = pltpu.roll(t[o], o, 1)
-            stay = stay + jnp.where(lane < o, 0.0, moved)
-            cross = cross + jnp.where(lane < o, moved, 0.0)
-        stay = jnp.where(low, stay + pltpu.roll(stay, HALF, 0), 0.0)
-        cross = jnp.where(low, cross + pltpu.roll(cross, HALF, 0), 0.0)
-        return stay + pltpu.roll(cross, 1, 0)
-
-    def end_part(self, v):
-        total = jnp.sum(v * self.ends, axis=1, keepdims=True)
-        return (total * (END_STIFF / 36.0)) * self.ends
+        return t
+
+    def shifted_sums(self, items):
+        lane, low = self.lane, self.low
+        outs = []
+        for i in range(0, len(items), 2):
+            one, two = items[i], items[i + 1] if i + 1 < len(items) else None
+            if two is None:
+                packed = [x + pltpu.roll(x, HALF, 0) for x in one]
+            else:
+                packed = [
+                    jnp.where(low, x, y) + pltpu.roll(jnp.where(low, y, x), HALF, 0)
+                    for x, y in zip(one, two)
+                ]
+            stay, cross = packed[0], None
+            for o in range(1, 4):
+                moved = pltpu.roll(packed[o], o, 1)
+                over = jnp.where(lane < o, moved, 0.0)
+                stay = stay + jnp.where(lane < o, 0.0, moved)
+                cross = over if cross is None else cross + over
+            outs.append(jnp.where(low, stay, 0.0) + pltpu.roll(jnp.where(low, cross, 0.0), 1, 0))
+            if two is not None:
+                carried = pltpu.roll(jnp.where(low, 0.0, cross), HALF + 1, 0)
+                outs.append(jnp.where(low, pltpu.roll(stay, HALF, 0), 0.0) + carried)
+        return outs
+
+    def end_parts(self, items):
+        outs = []
+        for i in range(0, len(items), HALF):
+            group = items[i : i + HALF]
+            rows = None
+            for j, v in enumerate(group):
+                row = v * self.ends if j == 0 else pltpu.roll(v * self.ends, j, 0)
+                rows = row if rows is None else rows + row
+            total = jnp.broadcast_to(jnp.sum(rows, axis=1, keepdims=True), (SUBS, LANES))
+            for j in range(len(group)):
+                turned = total if j == 0 else pltpu.roll(total, SUBS - j, 0)
+                outs.append(turned * self.springs)
+        return outs
 
     def line(self, name, column, h):
         return sum(MARKS[j] * self.take_ref[name, column + j, h] for j in range(3))
@@ -458,13 +504,12 @@
             ]
             second = [None, None, [acc_ref[F22, col, h] for h in halves]]
             work.append((zeroth, first, second, [load(col, i) for i in range(3)]))
-        return [
-            [
-                self.axial_put(zeroth[i], first[i], second[i]) + self.end_part(v[i])
-                for i in range(3)
-            ]
-            for zeroth, first, second, v in work
-        ]
+        sums = self.shifted_sums(
+            [self.axial_put(z[i], f[i], s[i]) for z, f, s, v in work for i in range(3)]
+        )
+        ends = self.end_parts([v[i] for z, f, s, v in work for i in range(3)])
+        images = [x + y for x, y in zip(sums, ends)]
+        return [images[i : i + 3] for i in range(0, len(images), 3)]
 
     def gather(self, low, high, load, image_ref, step, follow, carry, unroll, beyond=0):
         count = high - low
@@ -477,9 +522,8 @@
 
         def body(start, carry):
             cols = [start + ahead + u for u in range(unroll)]
-            images = self.image_columns(cols, load)
             carry = follow([start + u for u in range(unroll)], carry)
-            put(cols, images)
+            put(cols, self.image_columns(cols, load))
             return carry
 
         cols = list(range(low, low + ahead))
@@ -491,7 +535,9 @@
 
 
 def attached(source, shift):
-    return jnp.max(source[7:8, :]).astype(jnp.int32) + shift
+    row = source[7:8, :]
+    above = lax.broadcasted_iota(jnp.int32, row.shape, 1) >= ABOVE
+    return jnp.max(jnp.where(above, row, 0.0)).astype(jnp.int32) + shift
 
 
 def keep(ref, index, carry):
@@ -521,6 +567,7 @@
             field_ref[start : start + SUBS, :] = shell.zero
     shell.spread(own_ref, pad, own_cols)
     stop = pad + own_cols
+    shell.clear(pad - HALO, HALO)
 
     def state(col, index):
         return shell.field(col, (0, 1, 2, 6)[index])
@@ -547,6 +594,7 @@
     )
     keep(carry_ref, 2, carry)
     shell.acc_ref = second_ref
+    shell.clear(pad + 3 - HALO, HALO)
     shell.clear(pad + 3)
     shell.spans(pad + 3, stop - 6)
 
@@ -579,8 +627,9 @@
     shell = Shell(own_cols, pad, radius, field_ref, take_ref, acc_ref, state_ref, table_ref)
     field, zero = shell.field, shell.zero
     stop = pad + own_cols
-    shell.spread(left_ref, pad - HALO, HALO)
-    shell.spread(right_ref, stop, HALO)
+    for source, offset in ((left_ref, pad - HALO), (right_ref, stop)):
+        shell.spread(source, offset, HALO)
+        shell.spread_rests(source, offset, HALO)
 
     def carried(index):
         return tuple(tuple(carry_ref[index, h, i] for i in range(5)) for h in range(2))
@@ -642,7 +691,6 @@
             shell.axial_take(high, last + 3, load, VECTOR, carried(1))
         shell.acc_ref = second_ref if step == 1 else acc_ref
         if step < 2:
-            shell.clear(first, low - first)
             shell.spans(first, low, fresh=False)
             shell.spans(high - 3, last)
         else:
@@ -751,8 +799,8 @@
         functools.partial(pack_kernel, own_cols),
         out_shape=(
             shape(chunks * own_cols * SUBS, LANES),
-            shape(chunks * HALO * SUBS, LANES),
-            shape(chunks * HALO * SUBS, LANES),
+            shape((chunks - 1) * HALO * SUBS, LANES),
+            shape((chunks - 1) * HALO * SUBS, LANES),
         ),
         in_specs=[vmem, smem],
         out_specs=(vmem,) * 3,

time: 40.9 us -> 39.2 us (0.958)
  Pallas kernels: 23 us -> 21.3 us
    pallas_call x1, Pallas kernels: 15.4 us -> 13.9 us  [per_device(): pl.pallas_call(functools.partial(krylov_kernel, own_cols, pad, radius), o...]
where the time goes in v6:
time: 39.2 us; the launch traced here: 39 us
  Pallas kernels  21.3 us (54%)
  blocking collectives  9.85 us (25%)
  starting transfers between devices  5.59 us (14%)
  between operations  1.31 us (3%)
  other arithmetic  1.01 us (3%)
    pallas_call x1, Pallas kernels, per_device(): pl.pallas_call(functools.partial(krylov_kernel, own_cols, pad, radius), o...  13.9 us
    all_to_all x1, blocking collectives, per_device(): gram = lax.all_to_all(gram, 'circ', 0, 0, tiled=True)  9.85 us
    pallas_call x1, Pallas kernels, per_device(): pl.pallas_call(functools.partial(own_kernel, own_cols, pad, radius), out_...  5.65 us
    ppermute x1, starting transfers between devices, per_device(): lax.ppermute(head, 'circ', [((i + 1) % count, i) for i in range(count)])  5.05 us
    pallas_call x1, Pallas kernels, per_device(): pl.pallas_call(functools.partial(combine_kernel, count_all), out_shape=(s...  1.64 us
    concatenate x1, other arithmetic, per_device(): jnp.concatenate([state_field, direction, skin_thickness[None]], axis=0)  1.01 us
  transfers between devices with their start and end apart: 2, of which 0 were waited for; matrix products, arithmetic and copies ran while one was open for 0% of the time, Pallas kernels for 14%

profile of v6, /device:TPU:0, one launch (start us, length us, event | category | flops | bytes accessed | tf_op | source)
XLA Modules:
  0.0 39.0 jit_solution(16760337385452285875)
XLA Ops:
  1.3 1.0 %pad_maximum_fusion.fields_ref = f32[7,16,515]{2,1,0:T(8,128)S(1)} fusion(f32[1,16,515]{2,1,0:T(8,128)} %bitcast.7, f32[3,16,515]{2,1,0:T(8,128)} %param.5, f32[3,16,515]{2,1,0:T(8,128)} %param.4), kind=kLoop, calls=%fused_computation | loop fusion | flops 115360 | bytes 461440 | tf_op jit(solution)/shard_map/concatenate | solution.py:797
  2.3 0.1 pack.1
  2.4 0.5 %collective-permute-start = (f32[288,128]{1,0:T(8,128)S(1)}, f32[288,128]{1,0:T(8,128)S(1)}, u32[]{:S(2)}, u32[]{:S(2)}) collective-permute-start(f32[288,128]{1,0:T(8,128)S(1)} %get-tuple-element.15), channel_id=1, source_target_pairs={{0,1},{1,2},{2,3},{3,4},{4,5},{5,6},{6,7},{7,8},{8,9},{9,10},{10,1... | collective-permute-start | bytes 442376 | tf_op jit(solution)/shard_map/ppermute | solution.py:810
  3.0 5.0 %collective-permute-start.1 = (f32[288,128]{1,0:T(8,128)S(1)}, f32[288,128]{1,0:T(8,128)S(1)}, u32[]{:S(2)}, u32[]{:S(2)}) collective-permute-start(f32[288,128]{1,0:T(8,128)S(1)} %get-tuple-element.16), channel_id=1, source_target_pairs={{1,0},{2,1},{3,2},{4,3},{5,4},{6,5},{7,6},{8,7},{9,8},{10,9},{11,1... | collective-permute-start | bytes 442376 | tf_op jit(solution)/shard_map/ppermute | solution.py:811
  8.0 5.6 %own.1 = (f32[3072,128]{1,0:T(8,128)S(1)}, f32[21,48,2,8,128]{4,3,2,1,0:T(8,128)S(1)}, f32[10,48,2,8,128]{4,3,2,1,0:T(8,128)S(1)}, f32[10,48,2,8,128]{4,3,2,1,0:...) custom-call(f32[640,128]{1,0:T(8,128)S(1)} %get-tuple-element.17.own_ref), custom_call_target="tpu_custom_call" | custom-call | flops 40000000 | bytes 20000000 | tf_op jit(solution)/shard_map/own/pallas_call | solution.py:821
  13.7 0.0 collective-permute-done.left_ref
  13.7 0.0 collective-permute-done.1.right_ref
  13.7 13.9 %krylov.1 = (f32[4,384,128]{2,1,0:T(8,128)S(1)}, f32[16,128]{1,0:T(8,128)S(1)}, f32[3072,128]{1,0:T(8,128)S(1)}, f32[21,48,2,8,128]{4,3,2,1,0:T(8,128)S(1)}, f32...) custom-call(f32[288,128]{1,0:T(8,128)S(1)} %collective-permute-done., ...), custom_call_target="tpu_custom_call", output_to_operand_aliasing={{2}: (4, {}), {3}: (5, {}), {4}: (6, {}), {5}: (7, {}), {6}... | custom-call | tf_op jit(solution)/shard_map/krylov/pallas_call | solution.py:831
  27.5 9.8 %all_to_all.11 = f32[16,1,128]{2,1,0:T(1,128)S(1)} all-to-all(f32[16,1,128]{2,1,0:T(1,128)S(1)} %bitcast.6), channel_id=1, replica_groups=mesh['group'=2,'circ'=16] {'circ'}, dimensions={0} | all-to-all | bytes 16384 | tf_op jit(solution)/shard_map/all_to_all | solution.py:844
  37.4 1.6 %combine.1 = (f32[3,3,16,515]{3,2,1,0:T(8,128)}, f32[3]{0:T(128)}, f32[3]{0:T(128)}) custom-call(f32[16,128]{1,0:T(8,128)S(1)} %bitcast.5, f32[4,384,128]{2,1,0:T(8,128)S(1)} %get-tuple-element.26.krylov_ref), custom_call_target="tpu_custom_call" | custom-call | tf_op jit(solution)/shard_map/combine/pallas_call | solution.py:845
Async XLA Ops:
  2.4 11.2 %collective-permute-start = (f32[288,128]{1,0:T(8,128)S(1)}, f32[288,128]{1,0:T(8,128)S(1)}, u32[]{:S(2)}, u32[]{:S(2)}) collective-permute-start(f32[288,128]{1,0:T(8,128)S(1)} %get-tuple-element.15), channel_id=1, source_target_pairs={{0,1},{1,2},{2,3},{3,4},{4,5},{5,6},{6,7},{7,8},{8,9},{9,10},{10,1... | collective-permute-start | bytes 442376 | tf_op jit(solution)/shard_map/ppermute | solution.py:810
  3.0 10.7 %collective-permute-start.1 = (f32[288,128]{1,0:T(8,128)S(1)}, f32[288,128]{1,0:T(8,128)S(1)}, u32[]{:S(2)}, u32[]{:S(2)}) collective-permute-start(f32[288,128]{1,0:T(8,128)S(1)} %get-tuple-element.16), channel_id=1, source_target_pairs={{1,0},{2,1},{3,2},{4,3},{5,4},{6,5},{7,6},{8,7},{9,8},{10,9},{11,1... | collective-permute-start | bytes 442376 | tf_op jit(solution)/shard_map/ppermute | solution.py:811
